TPU v7x, 32 devices: a whole 2x2x4 slice. The times are simulated.
32 devices in a mesh: ctx: 8 (over z, core), head: 4 (over y, x).
Axes of the slice: x: 2, y: 2, z: 4, core: 2. Of those that a mesh axis runs over, the one named last changes fastest.
Arguments:
- query: bfloat16 [2048, 32, 128], P(('ctx', 'head')), may hold values from -6 to 6
- key: bfloat16 [2048, 16, 128], P(('ctx', 'head')), may hold values from -6 to 6
- value: bfloat16 [2048, 16, 128], P(('ctx', 'head')), may hold values from -6 to 6
- attn_out: bfloat16 [2048, 32, 128], P('ctx', 'head'), may hold values from -6 to 6
- out_grad: bfloat16 [2048, 32, 128], P(('ctx', 'head')), may hold values from -4 to 4
- lse: bfloat16 [32, 2048], P('head', 'ctx'), may hold values from 3 to 5
- doc_lengths: int32 [8], replicated, may hold values from 1 to 512, 2048 in all
Outputs:
- query_grad: bfloat16 [2048, 32, 128], P(('ctx', 'head'))
- key_grad: bfloat16 [2048, 16, 128], P(('ctx', 'head'))
- value_grad: bfloat16 [2048, 16, 128], P(('ctx', 'head'))
Inputs may be any that keep to these rules, and one draw needn't show every extreme that they name: `doc_lengths`: document lengths in the order of the packed sequence; they sum to 2048 and the largest is exactly 512.
All inputs are finite; a program needn't handle non-finite values.
Results may differ from a plain program's by a relative error of at most 0.0053.
Values may be sent and summed in bfloat16 or wider, within the bound.
No kernel may reach another device: no remote copies, remote signals or barrier semaphores. Data moves between devices by JAX's collectives and lax.ppermute only.
A program may use at most 64 MiB of HBM per device.

v0:
```python
import jax
import jax.numpy as jnp
from jax import lax
from jax.sharding import PartitionSpec as P

soft_cap = 50.0
score_scale = 144.0 ** (-0.5)


def shifted(value, axis, steps):
    count = lax.axis_size(axis)
    initial, last = (max(0, -steps), min(count, count - steps))
    return lax.ppermute(value, axis, [(source, source + steps) for source in range(initial, last)])


def doc_index(positions, doc_ends):
    return jnp.sum((positions[:, None] >= doc_ends[None, :]).astype(jnp.int32), axis=1)


def block_grads(queries, out_grads, lse_rows, delta_rows, key_rows, value_rows, allowed):
    raw_scores = jnp.einsum("tkgd,ukd->kgtu", queries, key_rows, preferred_element_type=jnp.float32)
    capped = soft_cap * jnp.tanh(raw_scores * (score_scale / soft_cap))
    weights = jnp.where(allowed[None, None], jnp.exp(capped - lse_rows[..., None]), 0.0)
    d_weights = jnp.einsum(
        "tkgd,ukd->kgtu", out_grads, value_rows, preferred_element_type=jnp.float32
    )
    d_scores = (
        weights
        * (d_weights - delta_rows[..., None])
        * (1.0 - (capped / soft_cap) ** 2)
        * score_scale
    ).astype(jnp.bfloat16)
    weights_low = weights.astype(jnp.bfloat16)
    d_query = jnp.einsum("kgtu,ukd->tkgd", d_scores, key_rows, preferred_element_type=jnp.float32)
    d_key = jnp.einsum("kgtu,tkgd->ukd", d_scores, queries, preferred_element_type=jnp.float32)
    d_value = jnp.einsum(
        "kgtu,tkgd->ukd", weights_low, out_grads, preferred_element_type=jnp.float32
    )
    return (d_query, jnp.stack([d_key, d_value], axis=2))


def advance(kv_block):
    return shifted(kv_block, "ctx", 1)


def per_device(query, key, value, attn_out, out_grad, lse, doc_lengths):
    far_blocks = min(6, lax.axis_size("ctx") // 4)
    tok_short, heads_all, head_width = query.shape
    kv_all = key.shape[1]
    per_group = heads_all // kv_all
    q_tokens = query.reshape(tok_short, kv_all, per_group, head_width)
    g_tokens = out_grad.reshape(tok_short, kv_all, per_group, head_width)
    kv_tokens = jnp.stack([key, value], axis=2)
    q_local, g_local, kv_local = (
        lax.all_to_all(q_tokens, "head", split_axis=1, concat_axis=0, tiled=True),
        lax.all_to_all(g_tokens, "head", split_axis=1, concat_axis=0, tiled=True),
        lax.all_to_all(kv_tokens, "head", split_axis=1, concat_axis=0, tiled=True),
    )
    tok_rows = q_local.shape[0]
    kv_here = q_local.shape[1]
    o_local = attn_out.reshape(tok_rows, kv_here, per_group, head_width)
    lse_rows = lse.astype(jnp.float32).reshape(kv_here, per_group, tok_rows)
    delta_rows = jnp.transpose(
        jnp.sum(g_local.astype(jnp.float32) * o_local.astype(jnp.float32), axis=-1), (1, 2, 0)
    )
    doc_ends = jnp.cumsum(doc_lengths)
    ctx_index = lax.axis_index("ctx")
    q_pos = ctx_index * tok_rows + jnp.arange(tok_rows, dtype=jnp.int32)
    q_doc = doc_index(q_pos, doc_ends)

    def visit_block(kv_block, behind):
        k_pos = (ctx_index - behind) * tok_rows + jnp.arange(tok_rows, dtype=jnp.int32)
        allowed = (
            (q_doc[:, None] == doc_index(k_pos, doc_ends)[None, :])
            & (k_pos[None, :] <= q_pos[:, None])
            & (k_pos[None, :] >= 0)
        )
        return block_grads(
            q_local, g_local, lse_rows, delta_rows, kv_block[:, :, 0], kv_block[:, :, 1], allowed
        )

    dq_sum, dkv_sum = visit_block(kv_local, 0)
    moving = kv_local
    for behind in range(1, far_blocks + 1):
        moving = advance(moving)
        dq_part, dkv_part = visit_block(moving, behind)
        dq_sum = dq_sum + dq_part
        dkv_sum = dkv_sum + shifted(dkv_part, "ctx", -behind)
    dq_back, dkv_back = (
        lax.all_to_all(
            dq_sum.astype(jnp.bfloat16), "head", split_axis=0, concat_axis=1, tiled=True
        ),
        lax.all_to_all(
            dkv_sum.astype(jnp.bfloat16), "head", split_axis=0, concat_axis=1, tiled=True
        ),
    )
    return (dq_back.reshape(tok_short, heads_all, head_width), dkv_back[:, :, 0], dkv_back[:, :, 1])


def solution(mesh):
    return jax.shard_map(
        per_device,
        mesh=mesh,
        in_specs=(
            P(("ctx", "head"), None, None),
            P(("ctx", "head"), None, None),
            P(("ctx", "head"), None, None),
            P("ctx", "head", None),
            P(("ctx", "head"), None, None),
            P("head", "ctx"),
            P(),
        ),
        out_specs=(
            P(("ctx", "head"), None, None),
            P(("ctx", "head"), None, None),
            P(("ctx", "head"), None, None),
        ),
        check_vma=False,
    )
```

profile of v0, /device:TPU:0, one launch (start us, length us, event | category | flops | bytes accessed | tf_op | source)
XLA Modules:
  0.0 104.9 jit_solution(10258983400603559710)
XLA Ops:
  0.6 1.2 %copy_bitcast_fusion = (bf16[64,16,1,128]{3,0,2,1:T(8,128)(2,1)S(1)}, bf16[64,16,1,128]{3,0,2,1:T(8,128)(2,1)S(1)}) fusion(bf16[64,16,128]{2,1,0:T(8,128)(2,1)} %param.9, bf16[64,16,128]{2,1,0:T(8,128)(2,1)} %param.8), kind=kLoop, calls=%fused_computation.68 | loop fusion | bytes 1048576 | tf_op jit(solution)/shard_map/stack | solution.py:53
  1.9 0.8 pad_maximum_fusion.2
  2.7 5.2 %all-to-all-start = ((bf16[64,16,2,128]{3,0,2,1:T(8,128)(2,1)}), bf16[64,16,2,128]{3,0,2,1:T(8,128)(2,1)S(1)}, u32[]{:S(2)}, u32[]{:S(2)}) async-start(bf16[64,16,2,128]{3,0,2,1:T(8,128)(2,1)} %pad_maximum_fusion.2), calls=%async_computation | async-start | bytes 1048576 | tf_op jit(solution)/shard_map/all_to_all | solution.py:57
  7.9 1.0 copy.96
  8.9 7.0 %all-to-all-done = bf16[64,16,2,128]{3,0,2,1:T(8,128)(2,1)S(1)} async-done(((bf16[64,16,2,128]{3,0,2,1:T(8,128)(2,1)}), bf16[64,16,2,128]{3,0,2,1:T(8,128)(2,1)S(1)}, u32[]{:S(2)}, u32[]{:S(2)}) %all-to-all-start) | async-done | bytes 524320 | tf_op jit(solution)/shard_map/all_to_all | solution.py:57
  15.9 3.6 %all-to-all-start.1 = ((bf16[64,16,2,128]{3,0,2,1:T(8,128)(2,1)}), bf16[64,16,2,128]{3,0,2,1:T(8,128)(2,1)S(1)}, u32[]{:S(2)}, u32[]{:S(2)}) async-start(bf16[64,16,2,128]{3,0,2,1:T(8,128)(2,1)} %bitcast.11), calls=%async_computation.1 | async-start | bytes 1048576 | tf_op jit(solution)/shard_map/all_to_all | solution.py:55
  19.6 1.0 copy.98
  20.6 6.1 %all-to-all-done.1 = bf16[64,16,2,128]{3,0,2,1:T(8,128)(2,1)S(1)} async-done(((bf16[64,16,2,128]{3,0,2,1:T(8,128)(2,1)}), bf16[64,16,2,128]{3,0,2,1:T(8,128)(2,1)S(1)}, u32[]{:S(2)}, u32[]{:S(2)}) %all-to-all-start.1) | async-done | bytes 524320 | tf_op jit(solution)/shard_map/all_to_all | solution.py:55
  26.7 3.5 %all-to-all-start.2 = ((bf16[64,16,2,128]{3,0,2,1:T(8,128)(2,1)}), bf16[64,16,2,128]{3,0,2,1:T(8,128)(2,1)S(1)}, u32[]{:S(2)}, u32[]{:S(2)}) async-start(bf16[64,16,2,128]{3,0,2,1:T(8,128)(2,1)} %bitcast.20), calls=%async_computation.2 | async-start | bytes 1048576 | tf_op jit(solution)/shard_map/all_to_all | solution.py:56
  31.2 2.1 %collective-permute-start = (bf16[256,4,2,128]{3,0,1,2:T(8,128)(2,1)S(1)}, bf16[256,4,2,128]{3,0,1,2:T(8,128)(2,1)}, u32[]{:S(2)}, u32[]{:S(2)}) collective-permute-start(bf16[256,4,2,128]{3,0,1,2:T(8,128)(2,1)S(1)} %bitcast.234), channel_id=1, source_target_pairs={{0,4},{4,8},{8,12},{12,16},{16,20},{20,24},{24,28},{1,5},{5,9},{9,... | collective-permute-start | bytes 1572872 | tf_op jit(solution)/shard_map/ppermute | solution.py:13
  33.3 3.4 %all-to-all-done.2 = bf16[64,16,2,128]{3,0,2,1:T(8,128)(2,1)S(1)} async-done(((bf16[64,16,2,128]{3,0,2,1:T(8,128)(2,1)}), bf16[64,16,2,128]{3,0,2,1:T(8,128)(2,1)S(1)}, u32[]{:S(2)}, u32[]{:S(2)}) %all-to-all-start.2) | async-done | bytes 524320 | tf_op jit(solution)/shard_map/all_to_all | solution.py:56
  37.2 0.7 convolution_bitcast_fusion.4
  39.0 2.7 %fusion.11 = bf16[4,2,256,256]{2,3,1,0:T(8,128)(2,1)S(1)} fusion(f32[4,256,256,2]{2,1,3,0:T(8,128)} %copy-done, bf16[256,4,2,128]{3,0,2,1:T(8,128)(2,1)S(1)} %bitcast.239, f32[4,2,256]{2,1,0:T(2,128)S(1)} %bitcast.244, f32[4,2,256]{2,1,0:T(2,128)S(1)} %reshape.294, pred[256,256]{0,1:T(8,128)(4,1)S(1)} %get-tuple-element.21, ...), kind=kOutput, calls=%fused_computation.18 | convolution fusion | flops 139984896 | bytes 4014080 | tf_op jit(solution)/shard_map/tkgd,ukd->kgtu/dot_general | solution.py:24
  41.7 1.4 %fusion.40 = f32[4,256,256,2]{2,1,3,0:T(8,128)S(1)} fusion(bf16[256,4,2,128]{3,0,2,1:T(8,128)(2,1)S(1)} %bitcast.220, bf16[256,4,2,128]{3,0,1,2:T(8,128)(2,1)} %collective-permute-done), kind=kOutput, calls=%fused_computation.75 | convolution fusion | flops 134217728 | bytes 2883584 | tf_op jit(solution)/shard_map/tkgd,ukd->kgtu/dot_general | solution.py:21
  43.1 1.3 %collective-permute-start.1 = (bf16[256,4,2,128]{3,0,1,2:T(8,128)(2,1)}, bf16[256,4,2,128]{3,0,1,2:T(8,128)(2,1)S(1)}, u32[]{:S(2)}, u32[]{:S(2)}) collective-permute-start(bf16[256,4,2,128]{3,0,1,2:T(8,128)(2,1)} %collective-permute-done), channel_id=1, source_target_pairs={{0,4},{4,8},{8,12},{12,16},{16,20},{20,24},{24,28},{1,5},{5,9},{9,... | collective-permute-start | bytes 1572872 | tf_op jit(solution)/shard_map/ppermute | solution.py:13
  44.4 2.1 %fusion.6 = bf16[4,2,256,256]{2,3,1,0:T(8,128)(2,1)S(1)} fusion(f32[4,256,256,2]{2,1,3,0:T(8,128)S(1)} %fusion.40, bf16[256,4,2,128]{3,0,2,1:T(8,128)(2,1)S(1)} %bitcast.240, f32[4,2,256]{2,1,0:T(2,128)S(1)} %bitcast.245, f32[4,2,256]{2,1,0:T(2,128)S(1)} %reshape.294, pred[256,256]{0,1:T(8,128)(4,1)S(1)} %get-tuple-element.22, ...), kind=kOutput, calls=%fused_computation.10 | convolution fusion | flops 139984896 | bytes 4014080 | tf_op jit(solution)/shard_map/tkgd,ukd->kgtu/dot_general | solution.py:24
  47.0 0.7 convolution_bitcast_fusion.2
  47.7 1.1 %pad_maximum_fusion = f32[256,4,2,128]{3,0,1,2:T(8,128)} fusion(f32[256,4,1,128]{3,0,1,2:T(8,128)S(1)} %convolution_bitcast_fusion.2, f32[256,4,1,128]{3,0,1,2:T(8,128)S(1)} %convolution_bitcast_fusion.3), kind=kLoop, calls=%fused_computation.43 | loop fusion | flops 262144 | bytes 2097152 | tf_op jit(solution)/shard_map/stack | solution.py:39
  48.7 1.3 %collective-permute-start.2 = (f32[256,4,2,128]{3,0,1,2:T(8,128)}, f32[256,4,2,128]{3,0,1,2:T(8,128)}, u32[]{:S(2)}, u32[]{:S(2)}) collective-permute-start(f32[256,4,2,128]{3,0,1,2:T(8,128)} %pad_maximum_fusion), channel_id=1, source_target_pairs={{4,0},{8,4},{12,8},{16,12},{20,16},{24,20},{28,24},{5,1},{9,5},{13... | collective-permute-start | bytes 3145736 | tf_op jit(solution)/shard_map/ppermute | solution.py:13
  51.2 1.1 %fusion.1 = bf16[4,2,256,256]{2,3,1,0:T(8,128)(2,1)S(1)} fusion(f32[4,256,256,2]{2,1,3,0:T(8,128)S(1)} %fusion.41, bf16[256,4,2,128]{3,0,2,1:T(8,128)(2,1)S(1)} %bitcast.243, f32[4,2,256]{2,1,0:T(2,128)S(1)} %bitcast.246, f32[4,2,256]{2,1,0:T(2,128)S(1)} %reshape.294, pred[256,256]{0,1:T(8,128)(4,1)S(1)} %get-tuple-element.20, ...), kind=kOutput, calls=%fused_computation.2 | convolution fusion | flops 139984896 | bytes 4014080 | tf_op jit(solution)/shard_map/tkgd,ukd->kgtu/dot_general | solution.py:24
  52.8 1.1 %pad_maximum_fusion.1 = f32[256,4,2,128]{3,0,1,2:T(8,128)} fusion(f32[256,4,1,128]{3,0,1,2:T(8,128)S(1)} %convolution_bitcast_fusion, f32[256,4,1,128]{3,0,1,2:T(8,128)S(1)} %convolution_bitcast_fusion.1), kind=kLoop, calls=%fused_computation.44 | loop fusion | flops 262144 | bytes 2097152 | tf_op jit(solution)/shard_map/stack | solution.py:39
  53.9 1.3 %collective-permute-start.3 = (f32[256,4,2,128]{3,0,1,2:T(8,128)}, f32[256,4,2,128]{3,0,1,2:T(8,128)}, u32[]{:S(2)}, u32[]{:S(2)}) collective-permute-start(f32[256,4,2,128]{3,0,1,2:T(8,128)} %pad_maximum_fusion.1), channel_id=1, source_target_pairs={{8,0},{12,4},{16,8},{20,12},{24,16},{28,20},{9,1},{13,5},{17,9},{2... | collective-permute-start | bytes 3145736 | tf_op jit(solution)/shard_map/ppermute | solution.py:13
  55.5 1.3 %convolution_add_fusion.1 = f32[4,128,2,256]{3,1,2,0:T(8,128)S(1)} fusion(f32[4,128,2,256]{3,1,2,0:T(8,128)S(1)} %fusion.39, bf16[4,2,256,256]{2,3,1,0:T(8,128)(2,1)S(1)} %fusion.6, bf16[256,4,2,128]{3,0,1,2:T(8,128)(2,1)} %collective-permute-done), kind=kOutput, calls=%fused_computation.31 | convolution fusion | flops 134479872 | bytes 3407872 | tf_op jit(solution)/shard_map/kgtu,ukd->tkgd/dot_general | solution.py:34
  57.1 1.2 %copy.109 = bf16[256,4,2,128]{3,2,1,0:T(2,128)(2,1)} copy(bf16[256,4,2,128]{0,3,2,1:T(8,128)(2,1)S(1)} %fusion.19) | data formatting | bytes 1048576 | tf_op jit(solution)/shard_map/convert_element_type | solution.py:91
  58.3 3.9 %all-to-all-start.3 = ((bf16[256,4,2,128]{3,2,1,0:T(2,128)(2,1)}), bf16[256,4,2,128]{3,2,1,0:T(2,128)(2,1)S(1)}, u32[]{:S(2)}, u32[]{:S(2)}) async-start(bf16[256,4,2,128]{3,2,1,0:T(2,128)(2,1)} %copy.109), calls=%async_computation.3 | async-start | bytes 1048576 | tf_op jit(solution)/shard_map/all_to_all | solution.py:90
  62.7 27.5 %collective-permute-done.3 = f32[256,4,2,128]{3,0,1,2:T(8,128)} collective-permute-done((f32[256,4,2,128]{3,0,1,2:T(8,128)}, f32[256,4,2,128]{3,0,1,2:T(8,128)}, u32[]{:S(2)}, u32[]{:S(2)}) %collective-permute-start.3) | collective-permute-done | bytes 1048608 | tf_op jit(solution)/shard_map/ppermute | solution.py:13
  90.2 1.7 %fusion.21 = bf16[256,4,2,128]{3,0,1,2:T(8,128)(2,1)S(1)} fusion(f32[256,4,2,128]{3,0,1,2:T(8,128)} %collective-permute-done.3, f32[256,4,2,128]{3,0,1,2:T(8,128)} %collective-permute-done.2, f32[256,4,1,128]{3,0,1,2:T(8,128)S(1)} %convolution_bitcast_fusion.4, f32[256,4,1,128]{3,0,1,2:T(8,128)S(1)} %convolution_bitcast_fusion.5), kind=kLoop, calls=%fused_computation.42 | loop fusion | flops 1048576 | bytes 3670016 | tf_op jit(solution)/shard_map/convert_element_type | solution.py:94
  91.9 1.2 %copy.112 = bf16[256,4,2,128]{3,1,2,0:T(4,128)(2,1)} copy(bf16[256,4,2,128]{3,0,1,2:T(8,128)(2,1)S(1)} %fusion.21) | data formatting | bytes 1048576 | tf_op jit(solution)/shard_map/convert_element_type | solution.py:94
  93.1 4.1 %all-to-all-start.4 = ((bf16[256,4,2,128]{3,1,2,0:T(4,128)(2,1)}), bf16[256,4,2,128]{3,1,2,0:T(4,128)(2,1)S(1)}, u32[]{:S(2)}, u32[]{:S(2)}) async-start(bf16[256,4,2,128]{3,1,2,0:T(4,128)(2,1)} %copy.112), calls=%async_computation.4 | async-start | bytes 1048576 | tf_op jit(solution)/shard_map/all_to_all | solution.py:93
  97.4 1.1 %copy.114 = bf16[64,32,128]{2,1,0:T(8,128)(2,1)} copy(bf16[64,32,128]{2,0,1:T(8,128)(2,1)S(1)} %bitcast.233) | data formatting | bytes 1048576
  98.5 5.3 %all-to-all-done.4 = bf16[256,4,2,128]{3,1,2,0:T(4,128)(2,1)S(1)} async-done(((bf16[256,4,2,128]{3,1,2,0:T(4,128)(2,1)}), bf16[256,4,2,128]{3,1,2,0:T(4,128)(2,1)S(1)}, u32[]{:S(2)}, u32[]{:S(2)}) %all-to-all-start.4) | async-done | bytes 524320 | tf_op jit(solution)/shard_map/all_to_all | solution.py:93
  104.0 0.8 slice_bitcast_fusion
  (42 shorter events, 5.9 us)
Async XLA Ops:
  0.6 7.3 %copy-start.1 = (bf16[64,32,128]{2,1,0:T(8,128)(2,1)S(1)}, bf16[64,32,128]{2,1,0:T(8,128)(2,1)}, u32[]{:S(2)}) copy-start(bf16[64,32,128]{2,1,0:T(8,128)(2,1)} %param.7) | copy-start | bytes 1572868
  1.9 17.7 %copy-start.2 = (bf16[64,32,128]{2,1,0:T(8,128)(2,1)S(1)}, bf16[64,32,128]{2,1,0:T(8,128)(2,1)}, u32[]{:S(2)}) copy-start(bf16[64,32,128]{2,1,0:T(8,128)(2,1)} %param.11) | copy-start | bytes 1572868
  2.7 13.2 %all-to-all-start = ((bf16[64,16,2,128]{3,0,2,1:T(8,128)(2,1)}), bf16[64,16,2,128]{3,0,2,1:T(8,128)(2,1)S(1)}, u32[]{:S(2)}, u32[]{:S(2)}) async-start(bf16[64,16,2,128]{3,0,2,1:T(8,128)(2,1)} %pad_maximum_fusion.2), calls=%async_computation | async-start | bytes 1048576 | tf_op jit(solution)/shard_map/all_to_all | solution.py:57
  7.9 22.3 %copy-start.4 = (bf16[8,256]{1,0:T(8,128)(2,1)S(1)}, bf16[8,256]{1,0:T(8,128)(2,1)}, u32[]{:S(2)}) copy-start(bf16[8,256]{1,0:T(8,128)(2,1)} %param.12) | copy-start | bytes 12292
  7.9 22.3 %copy-start.3 = (bf16[256,8,128]{2,1,0:T(8,128)(2,1)S(1)}, bf16[256,8,128]{2,1,0:T(8,128)(2,1)}, u32[]{:S(2)}) copy-start(bf16[256,8,128]{2,1,0:T(8,128)(2,1)} %param.10) | copy-start | bytes 1572868
  15.9 14.4 %copy-start.5 = (s32[8]{0:T(128)S(1)}, s32[8]{0:T(128)}, u32[]{:S(2)}) copy-start(s32[8]{0:T(128)} %param.13) | copy-start | bytes 100
  15.9 10.8 %all-to-all-start.1 = ((bf16[64,16,2,128]{3,0,2,1:T(8,128)(2,1)}), bf16[64,16,2,128]{3,0,2,1:T(8,128)(2,1)S(1)}, u32[]{:S(2)}, u32[]{:S(2)}) async-start(bf16[64,16,2,128]{3,0,2,1:T(8,128)(2,1)} %bitcast.11), calls=%async_computation.1 | async-start | bytes 1048576 | tf_op jit(solution)/shard_map/all_to_all | solution.py:55
  26.7 10.0 %all-to-all-start.2 = ((bf16[64,16,2,128]{3,0,2,1:T(8,128)(2,1)}), bf16[64,16,2,128]{3,0,2,1:T(8,128)(2,1)S(1)}, u32[]{:S(2)}, u32[]{:S(2)}) async-start(bf16[64,16,2,128]{3,0,2,1:T(8,128)(2,1)} %bitcast.20), calls=%async_computation.2 | async-start | bytes 1048576 | tf_op jit(solution)/shard_map/all_to_all | solution.py:56
  31.2 10.5 %collective-permute-start = (bf16[256,4,2,128]{3,0,1,2:T(8,128)(2,1)S(1)}, bf16[256,4,2,128]{3,0,1,2:T(8,128)(2,1)}, u32[]{:S(2)}, u32[]{:S(2)}) collective-permute-start(bf16[256,4,2,128]{3,0,1,2:T(8,128)(2,1)S(1)} %bitcast.234), channel_id=1, source_target_pairs={{0,4},{4,8},{8,12},{12,16},{16,20},{20,24},{24,28},{1,5},{5,9},{9,... | collective-permute-start | bytes 1572872 | tf_op jit(solution)/shard_map/ppermute | solution.py:13
  37.2 1.3 %copy-start = (f32[4,256,256,2]{2,1,3,0:T(8,128)}, f32[4,256,256,2]{2,1,3,0:T(8,128)S(1)}, u32[]{:S(2)}) copy-start(f32[4,256,256,2]{2,1,3,0:T(8,128)S(1)} %fusion.38) | copy-start | bytes 6291460
  43.1 6.9 %collective-permute-start.1 = (bf16[256,4,2,128]{3,0,1,2:T(8,128)(2,1)}, bf16[256,4,2,128]{3,0,1,2:T(8,128)(2,1)S(1)}, u32[]{:S(2)}, u32[]{:S(2)}) collective-permute-start(bf16[256,4,2,128]{3,0,1,2:T(8,128)(2,1)} %collective-permute-done), channel_id=1, source_target_pairs={{0,4},{4,8},{8,12},{12,16},{16,20},{20,24},{24,28},{1,5},{5,9},{9,... | collective-permute-start | bytes 1572872 | tf_op jit(solution)/shard_map/ppermute | solution.py:13
  48.7 13.9 %collective-permute-start.2 = (f32[256,4,2,128]{3,0,1,2:T(8,128)}, f32[256,4,2,128]{3,0,1,2:T(8,128)}, u32[]{:S(2)}, u32[]{:S(2)}) collective-permute-start(f32[256,4,2,128]{3,0,1,2:T(8,128)} %pad_maximum_fusion), channel_id=1, source_target_pairs={{4,0},{8,4},{12,8},{16,12},{20,16},{24,20},{28,24},{5,1},{9,5},{13... | collective-permute-start | bytes 3145736 | tf_op jit(solution)/shard_map/ppermute | solution.py:13
  53.9 36.3 %collective-permute-start.3 = (f32[256,4,2,128]{3,0,1,2:T(8,128)}, f32[256,4,2,128]{3,0,1,2:T(8,128)}, u32[]{:S(2)}, u32[]{:S(2)}) collective-permute-start(f32[256,4,2,128]{3,0,1,2:T(8,128)} %pad_maximum_fusion.1), channel_id=1, source_target_pairs={{8,0},{12,4},{16,8},{20,12},{24,16},{28,20},{9,1},{13,5},{17,9},{2... | collective-permute-start | bytes 3145736 | tf_op jit(solution)/shard_map/ppermute | solution.py:13
  58.3 34.8 %all-to-all-start.3 = ((bf16[256,4,2,128]{3,2,1,0:T(2,128)(2,1)}), bf16[256,4,2,128]{3,2,1,0:T(2,128)(2,1)S(1)}, u32[]{:S(2)}, u32[]{:S(2)}) async-start(bf16[256,4,2,128]{3,2,1,0:T(2,128)(2,1)} %copy.109), calls=%async_computation.3 | async-start | bytes 1048576 | tf_op jit(solution)/shard_map/all_to_all | solution.py:90
  93.1 10.7 %all-to-all-start.4 = ((bf16[256,4,2,128]{3,1,2,0:T(4,128)(2,1)}), bf16[256,4,2,128]{3,1,2,0:T(4,128)(2,1)S(1)}, u32[]{:S(2)}, u32[]{:S(2)}) async-start(bf16[256,4,2,128]{3,1,2,0:T(4,128)(2,1)} %copy.112), calls=%async_computation.4 | async-start | bytes 1048576 | tf_op jit(solution)/shard_map/all_to_all | solution.py:93
where the time goes:
time: 106 us; the launch traced here: 105 us
  waiting for transfers between devices  49.4 us (47%)
  starting transfers between devices  26.3 us (25%)
  matrix products  13.5 us (13%)
  local copies, waits for them, and re-layouts  8.75 us (8%)
  other arithmetic  5.94 us (6%)
    ppermute x4, waiting for transfers between devices, shifted(): lax.ppermute(value, axis, [(source, source + steps) for source in range(i...  27.5 us
    all_to_all x1, waiting for transfers between devices, per_device(): lax.all_to_all(kv_tokens, 'head', split_axis=1, concat_axis=0, tiled=True)  7 us
    all_to_all x1, waiting for transfers between devices, per_device(): lax.all_to_all(q_tokens, 'head', split_axis=1, concat_axis=0, tiled=True)  6.14 us
    ppermute x4, starting transfers between devices, shifted(): lax.ppermute(value, axis, [(source, source + steps) for source in range(i...  5.98 us
    dot_general x3, matrix products, block_grads(): jnp.einsum('tkgd,ukd->kgtu', out_grads, value_rows, preferred_element_typ...  5.91 us
    all_to_all x1, waiting for transfers between devices, per_device(): lax.all_to_all(dkv_sum.astype(jnp.bfloat16), 'head', split_axis=0, concat...  5.33 us
    all_to_all x1, starting transfers between devices, per_device(): lax.all_to_all(kv_tokens, 'head', split_axis=1, concat_axis=0, tiled=True)  5.19 us
    all_to_all x1, starting transfers between devices, per_device(): lax.all_to_all(dkv_sum.astype(jnp.bfloat16), 'head', split_axis=0, concat...  4.14 us
  transfers between devices with their start and end apart: 9, of which 5 were waited for; matrix products, arithmetic and copies ran while one was open for 22% of the time, Pallas kernels for 0%

commit v1 on v0

v1 whole, which is shorter than its diff:
```python
import functools
import math

import jax
import jax.numpy as jnp
from jax import lax
from jax.experimental import pallas as pl
from jax.experimental.pallas import tpu as pltpu
from jax.sharding import PartitionSpec as P

soft_cap = 50.0
score_scale = 144.0 ** (-0.5)
log2e = math.log2(math.e)


def swap_heads(value, step):
    count = lax.axis_size("head")
    return lax.ppermute(value, "head", [(i, i ^ step) for i in range(count)])


def rotate_ctx(value, steps):
    count = lax.axis_size("ctx")
    return lax.ppermute(value, "ctx", [(i, (i + steps) % count) for i in range(count)])


def swap_cores(value):
    count = lax.axis_size("ctx")
    return lax.ppermute(value, "ctx", [(i, i ^ 1) for i in range(count)])


def xor_order(blocks, index):
    count = blocks.shape[0]
    step = 1
    while step < count:
        swapped = blocks.reshape((count // (2 * step), 2, step) + blocks.shape[1:])[:, ::-1].reshape(blocks.shape)
        blocks = jnp.where((index & step) != 0, swapped, blocks)
        step *= 2
    return blocks


def dot(a, b, contract):
    return lax.dot_general(a, b, ((contract[0], contract[1]), ((), ())), preferred_element_type=jnp.float32)


NT = ((1,), (1,))
NN = ((1,), (0,))


def grads_kernel(planes, far, group, n_pieces, *refs):
    refs = list(refs)

    def take(n):
        out = refs[:n]
        del refs[:n]
        return out

    own_q, other_q = take(n_pieces), take(n_pieces)
    kv = [take(n_pieces) for _ in range(planes + 1)]
    own_o, other_o, own_lse, other_lse, own_start, other_start = take(6)
    dq_own, dq_other = take(n_pieces), take(n_pieces)
    dkv = [take(n_pieces) for _ in range(planes + 1)]
    acc_kv, acc_dq, ds_ref = take(3)

    rows, width = own_q[0].shape[2], own_q[0].shape[3]
    keys = rows * n_pieces
    ctx = lax.axis_index("ctx")
    head = lax.axis_index("head")
    core = ctx & 1

    acc_kv[...] = jnp.zeros_like(acc_kv)
    acc_dq[...] = jnp.zeros_like(acc_dq)

    def load_q(pieces, which):
        return jnp.concatenate([pieces[p][which, g] for g in range(group) for p in range(n_pieces)], axis=0)

    lane = lax.broadcasted_iota(jnp.int32, (1, group * keys), 1) % keys
    in_block = ((lane // rows) ^ head) * rows + lane % rows

    q_sets = []
    for pieces, o_ref, lse_ref, start_ref in (
        (own_q, own_o, own_lse, own_start),
        (other_q, other_o, other_lse, other_start),
    ):
        q_rows, g_rows = load_q(pieces, 0), load_q(pieces, 1)
        o_rows = o_ref[...].reshape(group * keys, width)
        prod = g_rows.astype(jnp.float32) * o_rows.astype(jnp.float32)
        high = prod.astype(jnp.bfloat16)
        low = (prod - high.astype(jnp.float32)).astype(jnp.bfloat16)
        ones = jnp.ones((8, width), jnp.bfloat16)
        delta = (dot(ones, high, NT) + dot(ones, low, NT))[0:1]
        q_sets.append((q_rows, g_rows, delta, lse_ref[0] * log2e, start_ref[...]))

    def pair(which_q, plane):
        q_rows, g_rows, delta, lse2, start = q_sets[which_q]
        key_ctx = ctx - 2 * plane
        for p in range(n_pieces):
            k_rows, v_rows = kv[plane][p][0, 0], kv[plane][p][1, 0]
            k_pos = key_ctx * keys + (head ^ p) * rows + lax.broadcasted_iota(jnp.int32, (rows, 1), 0)
            scores = dot(k_rows, q_rows, NT)
            d_weights = dot(v_rows, g_rows, NT)
            t = jnp.tanh(scores * (score_scale / soft_cap))
            weights = jnp.exp2(t * (soft_cap * log2e) - lse2)
            allowed = k_pos >= start
            if which_q == 0 and plane == 0:
                allowed = allowed & (k_pos <= ctx * keys + in_block)
            weights = jnp.where(allowed, weights, 0.0)
            d_scores = weights * (d_weights - delta) * ((1.0 - t * t) * score_scale)
            d_scores = d_scores.astype(jnp.bfloat16)
            ds_ref[pl.ds(p * rows, rows)] = d_scores
            span = pl.ds(p * rows, rows)
            acc_kv[plane, 0, span] += dot(d_scores, q_rows, NN)
            acc_kv[plane, 1, span] += dot(weights.astype(jnp.bfloat16), g_rows, NN)
        k_all = jnp.concatenate([kv[plane][p][0, 0] for p in range(n_pieces)], axis=0)
        acc_dq[which_q] += dot(k_all.T, ds_ref[...], NN)

    for plane in range(planes + 1):
        pair(0, plane)
        reached = ((core == 0) & (2 * plane + 1 <= far)) | ((core == 1) & (plane >= 1))
        pl.when(reached)(functools.partial(pair, 1, plane))

    for which_q, outs in ((0, dq_own), (1, dq_other)):
        full = acc_dq[which_q].T.reshape(group, n_pieces, rows, width)
        for p in range(n_pieces):
            outs[p][...] = full[:, p].astype(outs[p].dtype)
    for plane in range(planes + 1):
        for p in range(n_pieces):
            span = pl.ds(p * rows, rows)
            for which in range(2):
                dkv[plane][p][which, 0] = acc_kv[plane, which, span].astype(dkv[plane][p].dtype)


def grads_call(planes, far, group, own_q, other_q, kv, o_pair, lse_pair, start_pair):
    n_pieces = len(own_q)
    _, heads, rows, width = own_q[0].shape
    kv_heads = heads // group
    keys = rows * n_pieces
    f32, bf16 = jnp.float32, jnp.bfloat16
    q_spec = pl.BlockSpec((2, group, rows, width), lambda i: (0, i, 0, 0))
    kv_spec = pl.BlockSpec((2, 1, rows, width), lambda i: (0, i, 0, 0))
    o_spec = pl.BlockSpec((group, keys, width), lambda i: (i, 0, 0))
    lse_spec = pl.BlockSpec((1, 1, group * keys), lambda i: (i, 0, 0))
    start_spec = pl.BlockSpec((1, group * keys), lambda i: (0, 0))
    dq_spec = pl.BlockSpec((group, rows, width), lambda i: (i, 0, 0))
    shape = jax.ShapeDtypeStruct
    dq_shape, kv_shape = (heads, rows, width), (2, kv_heads, rows, width)
    pairs = kv_heads * 3 * planes * group
    outs = pl.pallas_call(
        functools.partial(grads_kernel, planes, far, group, n_pieces),
        grid=(kv_heads,),
        in_specs=[q_spec] * (2 * n_pieces) + [kv_spec] * ((planes + 1) * n_pieces) + [o_spec] * 2 + [lse_spec] * 2 + [start_spec] * 2,
        out_specs=[dq_spec] * (2 * n_pieces) + [kv_spec] * ((planes + 1) * n_pieces),
        out_shape=[shape(dq_shape, f32)] * n_pieces
        + [shape(dq_shape, bf16)] * n_pieces
        + [shape(kv_shape, f32)] * n_pieces
        + [shape(kv_shape, bf16)] * (planes * n_pieces),
        scratch_shapes=[
            pltpu.VMEM((planes + 1, 2, keys, width), f32),
            pltpu.VMEM((2, width, group * keys), f32),
            pltpu.VMEM((keys, group * keys), bf16),
        ],
        compiler_params=pltpu.CompilerParams(dimension_semantics=("arbitrary",), vmem_limit_bytes=24 * 1024 * 1024),
        cost_estimate=pl.CostEstimate(
            flops=pairs * 10 * keys * keys * width, bytes_accessed=8 * 1024 * 1024, transcendentals=pairs * 2 * keys * keys
        ),
        name="grads",
    )(*own_q, *other_q, *[piece for plane in kv for piece in plane], *o_pair, *lse_pair, *start_pair)
    chunks = [outs[i : i + n_pieces] for i in range(0, len(outs), n_pieces)]
    return chunks[0], chunks[1], chunks[2], chunks[3:]


def per_device(query, key, value, attn_out, out_grad, lse, doc_lengths):
    n_ctx, n_head = lax.axis_size("ctx"), lax.axis_size("head")
    far = min(6, n_ctx // 4)
    planes = (far + 1) // 2
    rows, heads_all, width = query.shape
    kv_all = key.shape[1]
    group = heads_all // kv_all
    ctx, head = lax.axis_index("ctx"), lax.axis_index("head")

    def piece(arrays, p):
        parts = []
        for x in arrays:
            blocks = x.reshape(rows, n_head, x.shape[1] // n_head, width)
            part = lax.dynamic_index_in_dim(blocks, head ^ p, 1, keepdims=False)
            parts.append(jnp.transpose(part, (1, 0, 2)))
        return jnp.stack(parts)

    kv_send = [piece((key, value), p) for p in range(n_head)]
    q_send = [piece((query, out_grad), p) for p in range(n_head)]
    exchange = lambda pieces: [pieces[0]] + [swap_heads(pieces[p], p) for p in range(1, n_head)]
    kv_own = exchange(kv_send)
    q_own = exchange(q_send)
    kv = [kv_own]
    for _ in range(planes):
        kv.append([rotate_ctx(piece_, 2) for piece_ in kv[-1]])
    q_other = [swap_cores(piece_) for piece_ in q_own]

    tok = rows * n_head
    heads_here = attn_out.shape[1]
    o_blocks = xor_order(attn_out.reshape(n_head, rows, heads_here, width), head)
    o_own = jnp.transpose(o_blocks, (2, 0, 1, 3)).reshape(heads_here, tok, width)
    o_other = swap_cores(o_own)
    lse_blocks = xor_order(jnp.transpose(lse.reshape(heads_here, n_head, rows), (1, 0, 2)), head)
    lse_own = jnp.transpose(lse_blocks, (1, 0, 2)).reshape(heads_here // group, 1, group * tok)
    lse_other = swap_cores(lse_own)

    doc_ends = jnp.cumsum(doc_lengths)

    def first_of_doc(block):
        lane = jnp.arange(tok, dtype=jnp.int32)
        pos = block * tok + ((lane // rows) ^ head) * rows + lane % rows
        start = jnp.max(jnp.where(doc_ends[None, :] <= pos[:, None], doc_ends[None, :], 0), axis=1)
        return jnp.tile(start, group)[None]

    dq_own, dq_other, dkv_own, dkv_far = grads_call(
        planes, far, group, q_own, q_other, kv,
        (o_own, o_other),
        (lse_own.astype(jnp.float32), lse_other.astype(jnp.float32)),
        (first_of_doc(ctx), first_of_doc(ctx ^ 1)),
    )
    f32, bf16 = jnp.float32, jnp.bfloat16
    dq_send = [(a + swap_cores(b).astype(f32)).astype(bf16) for a, b in zip(dq_own, dq_other)]
    back = dkv_far[planes - 1]
    for plane in range(planes - 1, 0, -1):
        moved = [rotate_ctx(x, -2) for x in back]
        back = [(a.astype(f32) + b.astype(f32)).astype(bf16) for a, b in zip(moved, dkv_far[plane - 1])]
    back = [rotate_ctx(x, -2) for x in back]
    dkv_send = [(a + b.astype(f32)).astype(bf16) for a, b in zip(dkv_own, back)]
    dq_back = xor_order(jnp.stack(exchange(dq_send)), head)
    dkv_back = xor_order(jnp.stack(exchange(dkv_send)), head)
    dq = jnp.transpose(dq_back, (2, 0, 1, 3)).reshape(rows, heads_all, width)
    dk = jnp.transpose(dkv_back[:, 0], (2, 0, 1, 3)).reshape(rows, kv_all, width)
    dv = jnp.transpose(dkv_back[:, 1], (2, 0, 1, 3)).reshape(rows, kv_all, width)
    return dq, dk, dv


def solution(mesh):
    return jax.shard_map(
        per_device,
        mesh=mesh,
        in_specs=(
            P(("ctx", "head"), None, None),
            P(("ctx", "head"), None, None),
            P(("ctx", "head"), None, None),
            P("ctx", "head", None),
            P(("ctx", "head"), None, None),
            P("head", "ctx"),
            P(),
        ),
        out_specs=(
            P(("ctx", "head"), None, None),
            P(("ctx", "head"), None, None),
            P(("ctx", "head"), None, None),
        ),
        check_vma=False,
    )
```

time: 106 us -> 72.2 us (0.68)
  waiting for transfers between devices: 49.4 us -> 13 us
  Pallas kernels: 0 us -> 16.6 us
  matrix products: 13.5 us -> 0 us
  starting transfers between devices: 26.3 us -> 30.3 us
  other arithmetic: 5.94 us -> 3.22 us
    ppermute x4 -> x30, starting transfers between devices: 5.98 us -> 30.3 us  [the longest x12 17 us: swap_heads(): return lax.ppermute(value, 'head', [(i, i ^ step) for i in range(count)])]
    all_to_all x5 -> x0, waiting for transfers between devices: 21.9 us -> none  [the longest x1 7 us: per_device(): lax.all_to_all(kv_tokens, 'head', split_axis=1, concat_axis=0, tiled=True)]
    all_to_all x5 -> x0, starting transfers between devices: 20.3 us -> none  [the longest x1 5.19 us: per_device(): lax.all_to_all(kv_tokens, 'head', split_axis=1, concat_axis=0, tiled=True)]
    pallas_call x0 -> x1, Pallas kernels: none -> 16.6 us  [grads_call(): pl.pallas_call(functools.partial(grads_kernel, planes, far, group, n_piec...]
    ppermute x4 -> x30, waiting for transfers between devices: 27.5 us -> 13 us  [the longest x8 7.86 us: rotate_ctx(): lax.ppermute(value, 'ctx', [(i, (i + steps) % count) for i in range(count)])]
    dot_general x15 -> x0, matrix products: 13.5 us -> none  [the longest x3 5.91 us: block_grads(): jnp.einsum('tkgd,ukd->kgtu', out_grads, value_rows, preferred_element_typ...]
    convert_element_type x2 -> x1, local copies, waits for them, and re-layouts: 2.37 us -> 0.01 us  [per_device(): lse_own.astype(jnp.float32)]
    another operation x4 -> x13, other arithmetic: 3.18 us -> 1.22 us  [the longest x8 0.82 us: piece(): return jnp.stack(parts)]
  transfers between devices with their start and end apart: 9 -> 30, of which waited for: 5 -> 10; matrix products, arithmetic and copies ran while one was open for 22% -> 8% of each run, Pallas kernels for 0% -> 0%
where the time goes in v1:
time: 72.2 us; the launch traced here: 71.9 us
  starting transfers between devices  30.3 us (42%)
  Pallas kernels  16.6 us (23%)
  waiting for transfers between devices  13 us (18%)
  local copies, waits for them, and re-layouts  7.7 us (11%)
  other arithmetic  3.22 us (4%)
  between operations  1.17 us (2%)
    ppermute x12, starting transfers between devices, swap_heads(): return lax.ppermute(value, 'head', [(i, i ^ step) for i in range(count)])  17 us
    pallas_call x1, Pallas kernels, grads_call(): pl.pallas_call(functools.partial(grads_kernel, planes, far, group, n_piec...  16.6 us
    ppermute x8, starting transfers between devices, rotate_ctx(): lax.ppermute(value, 'ctx', [(i, (i + steps) % count) for i in range(count)])  10.7 us
    ppermute x8, waiting for transfers between devices, rotate_ctx(): lax.ppermute(value, 'ctx', [(i, (i + steps) % count) for i in range(count)])  7.86 us
    unnamed x33, local copies, waits for them, and re-layouts  5.55 us
    ppermute x12, waiting for transfers between devices, swap_heads(): return lax.ppermute(value, 'head', [(i, i ^ step) for i in range(count)])  4.47 us
    ppermute x10, starting transfers between devices, swap_cores(): return lax.ppermute(value, 'ctx', [(i, i ^ 1) for i in range(count)])  2.58 us
  transfers between devices with their start and end apart: 30, of which 10 were waited for; matrix products, arithmetic and copies ran while one was open for 8% of the time, Pallas kernels for 0%

profile of v1, /device:TPU:0, one launch (start us, length us, event | category | flops | bytes accessed | tf_op | source)
XLA Modules:
  0.0 71.9 jit_solution(1708390647669916658)
XLA Ops:
  0.6 0.7 copy-done.3
  1.6 0.6 collective-permute-start.15
  2.2 1.2 %constant_dynamic-slice_fusion = (bf16[64,1,4,128]{3,2,1,0:T(4,128)(2,1)S(1)}, bf16[64,1,4,128]{3,2,1,0:T(4,128)(2,1)S(1)}, bf16[64,1,4,128]{3,2,1,0:T(4,128)(2,...) fusion(bf16[64,4,4,128]{3,2,1,0:T(4,128)(2,1)} %bitcast.237, ...), kind=kLoop, calls=%fused_computation.49 | loop fusion | bytes 1048592 | tf_op jit(solution)/shard_map/jit(dynamic_index_in_dim)/dynamic_slice | solution.py:184
  3.5 3.5 %collective-permute-start.9 = (bf16[2,4,64,128]{3,2,1,0:T(8,128)(2,1)S(1)}, bf16[2,4,64,128]{3,2,1,0:T(8,128)(2,1)S(1)}, u32[]{:S(2)}, u32[]{:S(2)}) collective-permute-start(bf16[2,4,64,128]{3,2,1,0:T(8,128)(2,1)S(1)} %pad_maximum_fusion.9), channel_id=1, source_target_pairs={{0,3},{1,2},{2,1},{3,0},{4,7},{5,6},{6,5},{7,4},{8,11},{9,10},{10,... | collective-permute-start | bytes 393224 | tf_op jit(solution)/shard_map/ppermute | solution.py:18
  7.1 0.6 collective-permute-start.8
  7.7 0.7 pad_maximum_fusion.7
  8.5 2.1 %collective-permute-start.10 = (bf16[2,4,64,128]{3,2,1,0:T(8,128)(2,1)S(1)}, bf16[2,4,64,128]{3,2,1,0:T(8,128)(2,1)S(1)}, u32[]{:S(2)}, u32[]{:S(2)}) collective-permute-start(bf16[2,4,64,128]{3,2,1,0:T(8,128)(2,1)S(1)} %pad_maximum_fusion.6.refs_8_), channel_id=1, source_target_pairs={{0,8},{4,12},{8,16},{12,20},{16,24},{20,28},{24,0},{28,4},{1,9},{5... | collective-permute-start | bytes 393224 | tf_op jit(solution)/shard_map/ppermute | solution.py:23
  11.1 0.9 %copy-done.1 = bf16[64,32,128]{2,1,0:T(8,128)(2,1)S(1)} copy-done((bf16[64,32,128]{2,1,0:T(8,128)(2,1)S(1)}, bf16[64,32,128]{2,1,0:T(8,128)(2,1)}, u32[]{:S(2)}) %copy-start.1) | copy-done | bytes 524312
  12.7 1.6 %collective-permute-start.13 = (bf16[2,4,64,128]{3,2,1,0:T(8,128)(2,1)S(1)}, bf16[2,4,64,128]{3,2,1,0:T(8,128)(2,1)S(1)}, u32[]{:S(2)}, u32[]{:S(2)}) collective-permute-start(bf16[2,4,64,128]{3,2,1,0:T(8,128)(2,1)S(1)} %collective-permute-done.9.refs_11_), channel_id=1, source_target_pairs={{0,8},{4,12},{8,16},{12,20},{16,24},{20,28},{24,0},{28,4},{1,9},{5... | collective-permute-start | bytes 393224 | tf_op jit(solution)/shard_map/ppermute | solution.py:23
  14.4 2.5 %collective-permute-start.2 = (bf16[2,8,64,128]{3,2,1,0:T(8,128)(2,1)S(1)}, bf16[2,8,64,128]{3,2,1,0:T(8,128)(2,1)S(1)}, u32[]{:S(2)}, u32[]{:S(2)}) collective-permute-start(bf16[2,8,64,128]{3,2,1,0:T(8,128)(2,1)S(1)} %pad_maximum_fusion.5), channel_id=1, source_target_pairs={{0,3},{1,2},{2,1},{3,0},{4,7},{5,6},{6,5},{7,4},{8,11},{9,10},{10,... | collective-permute-start | bytes 786440 | tf_op jit(solution)/shard_map/ppermute | solution.py:18
  18.0 1.6 %collective-permute-start.12 = (bf16[2,4,64,128]{3,2,1,0:T(8,128)(2,1)S(1)}, bf16[2,4,64,128]{3,2,1,0:T(8,128)(2,1)S(1)}, u32[]{:S(2)}, u32[]{:S(2)}) collective-permute-start(bf16[2,4,64,128]{3,2,1,0:T(8,128)(2,1)S(1)} %collective-permute-done.8.refs_10_), channel_id=1, source_target_pairs={{0,8},{4,12},{8,16},{12,20},{16,24},{20,28},{24,0},{28,4},{1,9},{5... | collective-permute-start | bytes 393224 | tf_op jit(solution)/shard_map/ppermute | solution.py:23
  20.0 0.7 copy-done.4
  20.8 4.1 %collective-permute-done.12.refs_14_ = bf16[2,4,64,128]{3,2,1,0:T(8,128)(2,1)S(1)} collective-permute-done((bf16[2,4,64,128]{3,2,1,0:T(8,128)(2,1)S(1)}, bf16[2,4,64,128]{3,2,1,0:T(8,128)(2,1)S(1)}, u32[]{:S(2)}, u32[]{:S(2)}) %collective-permute-start.12) | collective-permute-done | bytes 131104 | tf_op jit(solution)/shard_map/ppermute | solution.py:23
  25.0 1.4 %collective-permute-done.11.refs_13_ = bf16[2,4,64,128]{3,2,1,0:T(8,128)(2,1)S(1)} collective-permute-done((bf16[2,4,64,128]{3,2,1,0:T(8,128)(2,1)S(1)}, bf16[2,4,64,128]{3,2,1,0:T(8,128)(2,1)S(1)}, u32[]{:S(2)}, u32[]{:S(2)}) %collective-permute-start.11) | collective-permute-done | bytes 131104 | tf_op jit(solution)/shard_map/ppermute | solution.py:23
  26.9 1.3 %collective-permute-done.1.refs_2_ = bf16[2,8,64,128]{3,2,1,0:T(8,128)(2,1)S(1)} collective-permute-done((bf16[2,8,64,128]{3,2,1,0:T(8,128)(2,1)S(1)}, bf16[2,8,64,128]{3,2,1,0:T(8,128)(2,1)S(1)}, u32[]{:S(2)}, u32[]{:S(2)}) %collective-permute-start.1) | collective-permute-done | bytes 262176 | tf_op jit(solution)/shard_map/ppermute | solution.py:18
  28.8 0.7 convert_element_type.55.refs_19_
  30.2 16.6 %grads.1 = (f32[8,64,128]{2,1,0:T(8,128)S(1)}, f32[8,64,128]{2,1,0:T(8,128)S(1)}, f32[8,64,128]{2,1,0:T(8,128)S(1)}, f32[8,64,128]{2,1,0:T(8,128)S(1)}, bf16[8,6...) custom-call(bf16[2,8,64,128]{3,2,1,0:T(8,128)(2,1)S(1)} %pad_maximum, ...), custom_call_target="tpu_custom_call" | custom-call | flops 2013265920 | bytes 8388608 | tf_op jit(solution)/shard_map/grads/pallas_call | solution.py:147
  47.9 2.2 %collective-permute-start.23 = (bf16[2,4,64,128]{3,2,1,0:T(8,128)(2,1)S(1)}, bf16[2,4,64,128]{3,2,1,0:T(8,128)(2,1)S(1)}, u32[]{:S(2)}, u32[]{:S(2)}) collective-permute-start(bf16[2,4,64,128]{3,2,1,0:T(8,128)(2,1)S(1)} %get-tuple-element.28), channel_id=1, source_target_pairs={{0,24},{4,28},{8,0},{12,4},{16,8},{20,12},{24,16},{28,20},{1,25},{... | collective-permute-start | bytes 393224 | tf_op jit(solution)/shard_map/ppermute | solution.py:23
  50.1 0.7 collective-permute-start.24
  50.8 1.7 %collective-permute-start.26 = (bf16[2,4,64,128]{3,2,1,0:T(8,128)(2,1)S(1)}, bf16[2,4,64,128]{3,2,1,0:T(8,128)(2,1)S(1)}, u32[]{:S(2)}, u32[]{:S(2)}) collective-permute-start(bf16[2,4,64,128]{3,2,1,0:T(8,128)(2,1)S(1)} %get-tuple-element.32), channel_id=1, source_target_pairs={{0,24},{4,28},{8,0},{12,4},{16,8},{20,12},{24,16},{28,20},{1,25},{... | collective-permute-start | bytes 393224 | tf_op jit(solution)/shard_map/ppermute | solution.py:23
  53.1 1.6 %collective-permute-start.18 = (bf16[8,64,128]{2,1,0:T(8,128)(2,1)S(1)}, bf16[8,64,128]{2,1,0:T(8,128)(2,1)S(1)}, u32[]{:S(2)}, u32[]{:S(2)}) collective-permute-start(bf16[8,64,128]{2,1,0:T(8,128)(2,1)S(1)} %add_convert_fusion.6), channel_id=1, source_target_pairs={{0,1},{1,0},{2,3},{3,2},{4,5},{5,4},{6,7},{7,6},{8,9},{9,8},{10,11... | collective-permute-start | bytes 393224 | tf_op jit(solution)/shard_map/ppermute | solution.py:18
  54.7 1.1 %collective-permute-start.20 = (bf16[8,64,128]{2,1,0:T(8,128)(2,1)S(1)}, bf16[8,64,128]{2,1,0:T(8,128)(2,1)S(1)}, u32[]{:S(2)}, u32[]{:S(2)}) collective-permute-start(bf16[8,64,128]{2,1,0:T(8,128)(2,1)S(1)} %add_convert_fusion.5), channel_id=1, source_target_pairs={{0,2},{1,3},{2,0},{3,1},{4,6},{5,7},{6,4},{7,5},{8,10},{9,11},{10,... | collective-permute-start | bytes 393224 | tf_op jit(solution)/shard_map/ppermute | solution.py:18
  55.8 1.2 %collective-permute-done.24 = bf16[2,4,64,128]{3,2,1,0:T(8,128)(2,1)S(1)} collective-permute-done((bf16[2,4,64,128]{3,2,1,0:T(8,128)(2,1)S(1)}, bf16[2,4,64,128]{3,2,1,0:T(8,128)(2,1)S(1)}, u32[]{:S(2)}, u32[]{:S(2)}) %collective-permute-start.24) | collective-permute-done | bytes 131104 | tf_op jit(solution)/shard_map/ppermute | solution.py:23
  57.0 2.1 %collective-permute-start.22 = (bf16[8,64,128]{2,1,0:T(8,128)(2,1)S(1)}, bf16[8,64,128]{2,1,0:T(8,128)(2,1)S(1)}, u32[]{:S(2)}, u32[]{:S(2)}) collective-permute-start(bf16[8,64,128]{2,1,0:T(8,128)(2,1)S(1)} %add_convert_fusion.4), channel_id=1, source_target_pairs={{0,3},{1,2},{2,1},{3,0},{4,7},{5,6},{6,5},{7,4},{8,11},{9,10},{10,... | collective-permute-start | bytes 393224 | tf_op jit(solution)/shard_map/ppermute | solution.py:18
  59.2 0.7 collective-permute-done.26
  59.8 1.5 %collective-permute-start.25 = (bf16[2,4,64,128]{3,2,1,0:T(8,128)(2,1)S(1)}, bf16[2,4,64,128]{3,2,1,0:T(8,128)(2,1)S(1)}, u32[]{:S(2)}, u32[]{:S(2)}) collective-permute-start(bf16[2,4,64,128]{3,2,1,0:T(8,128)(2,1)S(1)} %add_convert_fusion.2), channel_id=1, source_target_pairs={{0,1},{1,0},{2,3},{3,2},{4,5},{5,4},{6,7},{7,6},{8,9},{9,8},{10,11... | collective-permute-start | bytes 393224 | tf_op jit(solution)/shard_map/ppermute | solution.py:18
  61.8 1.5 %collective-permute-start.27 = (bf16[2,4,64,128]{3,2,1,0:T(8,128)(2,1)S(1)}, bf16[2,4,64,128]{3,2,1,0:T(8,128)(2,1)S(1)}, u32[]{:S(2)}, u32[]{:S(2)}) collective-permute-start(bf16[2,4,64,128]{3,2,1,0:T(8,128)(2,1)S(1)} %add_convert_fusion.1), channel_id=1, source_target_pairs={{0,2},{1,3},{2,0},{3,1},{4,6},{5,7},{6,4},{7,5},{8,10},{9,11},{10,... | collective-permute-start | bytes 393224 | tf_op jit(solution)/shard_map/ppermute | solution.py:18
  63.4 1.5 %collective-permute-start.29 = (bf16[2,4,64,128]{3,2,1,0:T(8,128)(2,1)S(1)}, bf16[2,4,64,128]{3,2,1,0:T(8,128)(2,1)S(1)}, u32[]{:S(2)}, u32[]{:S(2)}) collective-permute-start(bf16[2,4,64,128]{3,2,1,0:T(8,128)(2,1)S(1)} %add_convert_fusion), channel_id=1, source_target_pairs={{0,3},{1,2},{2,1},{3,0},{4,7},{5,6},{6,5},{7,4},{8,11},{9,10},{10,... | collective-permute-start | bytes 393224 | tf_op jit(solution)/shard_map/ppermute | solution.py:18
  65.4 1.1 %copy.101 = bf16[64,32,128]{2,1,0:T(8,128)(2,1)} copy(bf16[64,32,128]{2,0,1:T(8,128)(2,1)S(1)} %bitcast.204) | data formatting | bytes 1048576
  66.6 3.0 %collective-permute-done.27 = bf16[2,4,64,128]{3,2,1,0:T(8,128)(2,1)S(1)} collective-permute-done((bf16[2,4,64,128]{3,2,1,0:T(8,128)(2,1)S(1)}, bf16[2,4,64,128]{3,2,1,0:T(8,128)(2,1)S(1)}, u32[]{:S(2)}, u32[]{:S(2)}) %collective-permute-start.27) | collective-permute-done | bytes 131104 | tf_op jit(solution)/shard_map/ppermute | solution.py:18
  70.2 0.9 %copy.103 = bf16[64,16,128]{2,1,0:T(8,128)(2,1)} copy(bf16[64,16,128]{2,0,1:T(8,128)(2,1)S(1)} %bitcast.206) | data formatting | bytes 524288
  71.1 0.9 %copy.102 = bf16[64,16,128]{2,1,0:T(8,128)(2,1)} copy(bf16[64,16,128]{2,0,1:T(8,128)(2,1)S(1)} %bitcast.205) | data formatting | bytes 524288
  (109 shorter events, 8.4 us)
Async XLA Ops:
  1.6 12.8 %collective-permute-start.15 = (bf16[4,1,512]{2,1,0:T(2,128)(2,1)S(1)}, bf16[4,1,512]{2,1,0:T(2,128)(2,1)}, u32[]{:S(2)}, u32[]{:S(2)}) collective-permute-start(bf16[4,1,512]{2,1,0:T(2,128)(2,1)S(1)} %copy.99), channel_id=1, source_target_pairs={{0,4},{4,0},{8,12},{12,8},{16,20},{20,16},{24,28},{28,24},{1,5},{5... | collective-permute-start | bytes 12296 | tf_op jit(solution)/shard_map/ppermute | solution.py:28
  3.5 9.2 %collective-permute-start.9 = (bf16[2,4,64,128]{3,2,1,0:T(8,128)(2,1)S(1)}, bf16[2,4,64,128]{3,2,1,0:T(8,128)(2,1)S(1)}, u32[]{:S(2)}, u32[]{:S(2)}) collective-permute-start(bf16[2,4,64,128]{3,2,1,0:T(8,128)(2,1)S(1)} %pad_maximum_fusion.9), channel_id=1, source_target_pairs={{0,3},{1,2},{2,1},{3,0},{4,7},{5,6},{6,5},{7,4},{8,11},{9,10},{10,... | collective-permute-start | bytes 393224 | tf_op jit(solution)/shard_map/ppermute | solution.py:18
  7.1 9.9 %collective-permute-start.8 = (bf16[2,4,64,128]{3,2,1,0:T(8,128)(2,1)S(1)}, bf16[2,4,64,128]{3,2,1,0:T(8,128)(2,1)S(1)}, u32[]{:S(2)}, u32[]{:S(2)}) collective-permute-start(bf16[2,4,64,128]{3,2,1,0:T(8,128)(2,1)S(1)} %pad_maximum_fusion.8), channel_id=1, source_target_pairs={{0,2},{1,3},{2,0},{3,1},{4,6},{5,7},{6,4},{7,5},{8,10},{9,11},{10,... | collective-permute-start | bytes 393224 | tf_op jit(solution)/shard_map/ppermute | solution.py:18
  7.6 2.9 %copy-start = (bf16[256,8,128]{2,1,0:T(8,128)(2,1)S(1)}, bf16[256,8,128]{2,1,0:T(8,128)(2,1)}, u32[]{:S(2)}) copy-start(bf16[256,8,128]{2,1,0:T(8,128)(2,1)} %param.10) | copy-start | bytes 1572868
  8.3 9.1 %collective-permute-start.7 = (bf16[2,4,64,128]{3,2,1,0:T(8,128)(2,1)}, bf16[2,4,64,128]{3,2,1,0:T(8,128)(2,1)S(1)}, u32[]{:S(2)}, u32[]{:S(2)}) collective-permute-start(bf16[2,4,64,128]{3,2,1,0:T(8,128)(2,1)} %pad_maximum_fusion.7), channel_id=1, source_target_pairs={{0,1},{1,0},{2,3},{3,2},{4,5},{5,4},{6,7},{7,6},{8,9},{9,8},{10,11... | collective-permute-start | bytes 393224 | tf_op jit(solution)/shard_map/ppermute | solution.py:18
  8.5 9.5 %collective-permute-start.10 = (bf16[2,4,64,128]{3,2,1,0:T(8,128)(2,1)S(1)}, bf16[2,4,64,128]{3,2,1,0:T(8,128)(2,1)S(1)}, u32[]{:S(2)}, u32[]{:S(2)}) collective-permute-start(bf16[2,4,64,128]{3,2,1,0:T(8,128)(2,1)S(1)} %pad_maximum_fusion.6.refs_8_), channel_id=1, source_target_pairs={{0,8},{4,12},{8,16},{12,20},{16,24},{20,28},{24,0},{28,4},{1,9},{5... | collective-permute-start | bytes 393224 | tf_op jit(solution)/shard_map/ppermute | solution.py:23
  10.9 1.2 %copy-start.2 = (bf16[64,32,128]{2,1,0:T(8,128)(2,1)S(1)}, bf16[64,32,128]{2,1,0:T(8,128)(2,1)}, u32[]{:S(2)}) copy-start(bf16[64,32,128]{2,1,0:T(8,128)(2,1)} %param.7) | copy-start | bytes 1572868
  12.7 6.9 %collective-permute-start.13 = (bf16[2,4,64,128]{3,2,1,0:T(8,128)(2,1)S(1)}, bf16[2,4,64,128]{3,2,1,0:T(8,128)(2,1)S(1)}, u32[]{:S(2)}, u32[]{:S(2)}) collective-permute-start(bf16[2,4,64,128]{3,2,1,0:T(8,128)(2,1)S(1)} %collective-permute-done.9.refs_11_), channel_id=1, source_target_pairs={{0,8},{4,12},{8,16},{12,20},{16,24},{20,28},{24,0},{28,4},{1,9},{5... | collective-permute-start | bytes 393224 | tf_op jit(solution)/shard_map/ppermute | solution.py:23
  14.4 12.0 %collective-permute-start.2 = (bf16[2,8,64,128]{3,2,1,0:T(8,128)(2,1)S(1)}, bf16[2,8,64,128]{3,2,1,0:T(8,128)(2,1)S(1)}, u32[]{:S(2)}, u32[]{:S(2)}) collective-permute-start(bf16[2,8,64,128]{3,2,1,0:T(8,128)(2,1)S(1)} %pad_maximum_fusion.5), channel_id=1, source_target_pairs={{0,3},{1,2},{2,1},{3,0},{4,7},{5,6},{6,5},{7,4},{8,11},{9,10},{10,... | collective-permute-start | bytes 786440 | tf_op jit(solution)/shard_map/ppermute | solution.py:18
  16.9 11.3 %collective-permute-start.1 = (bf16[2,8,64,128]{3,2,1,0:T(8,128)(2,1)S(1)}, bf16[2,8,64,128]{3,2,1,0:T(8,128)(2,1)S(1)}, u32[]{:S(2)}, u32[]{:S(2)}) collective-permute-start(bf16[2,8,64,128]{3,2,1,0:T(8,128)(2,1)S(1)} %pad_maximum_fusion.4), channel_id=1, source_target_pairs={{0,2},{1,3},{2,0},{3,1},{4,6},{5,7},{6,4},{7,5},{8,10},{9,11},{10,... | collective-permute-start | bytes 786440 | tf_op jit(solution)/shard_map/ppermute | solution.py:18
  17.4 10.9 %collective-permute-start = (bf16[2,8,64,128]{3,2,1,0:T(8,128)(2,1)S(1)}, bf16[2,8,64,128]{3,2,1,0:T(8,128)(2,1)S(1)}, u32[]{:S(2)}, u32[]{:S(2)}) collective-permute-start(bf16[2,8,64,128]{3,2,1,0:T(8,128)(2,1)S(1)} %pad_maximum_fusion.3), channel_id=1, source_target_pairs={{0,1},{1,0},{2,3},{3,2},{4,5},{5,4},{6,7},{7,6},{8,9},{9,8},{10,11... | collective-permute-start | bytes 786440 | tf_op jit(solution)/shard_map/ppermute | solution.py:18
  18.0 6.9 %collective-permute-start.12 = (bf16[2,4,64,128]{3,2,1,0:T(8,128)(2,1)S(1)}, bf16[2,4,64,128]{3,2,1,0:T(8,128)(2,1)S(1)}, u32[]{:S(2)}, u32[]{:S(2)}) collective-permute-start(bf16[2,4,64,128]{3,2,1,0:T(8,128)(2,1)S(1)} %collective-permute-done.8.refs_10_), channel_id=1, source_target_pairs={{0,8},{4,12},{8,16},{12,20},{16,24},{20,28},{24,0},{28,4},{1,9},{5... | collective-permute-start | bytes 393224 | tf_op jit(solution)/shard_map/ppermute | solution.py:23
  19.6 6.8 %collective-permute-start.11 = (bf16[2,4,64,128]{3,2,1,0:T(8,128)(2,1)S(1)}, bf16[2,4,64,128]{3,2,1,0:T(8,128)(2,1)S(1)}, u32[]{:S(2)}, u32[]{:S(2)}) collective-permute-start(bf16[2,4,64,128]{3,2,1,0:T(8,128)(2,1)S(1)} %collective-permute-done.7.refs_9_), channel_id=1, source_target_pairs={{0,8},{4,12},{8,16},{12,20},{16,24},{20,28},{24,0},{28,4},{1,9},{5... | collective-permute-start | bytes 393224 | tf_op jit(solution)/shard_map/ppermute | solution.py:23
  24.9 4.7 %collective-permute-start.14 = (bf16[8,256,128]{2,1,0:T(8,128)(2,1)S(1)}, bf16[8,256,128]{2,1,0:T(8,128)(2,1)S(1)}, u32[]{:S(2)}, u32[]{:S(2)}) collective-permute-start(bf16[8,256,128]{2,1,0:T(8,128)(2,1)S(1)} %bitcast.188), channel_id=1, source_target_pairs={{0,4},{4,0},{8,12},{12,8},{16,20},{20,16},{24,28},{28,24},{1,5},{5... | collective-permute-start | bytes 1572872 | tf_op jit(solution)/shard_map/ppermute | solution.py:28
  26.4 3.1 %collective-permute-start.3 = (bf16[2,8,64,128]{3,2,1,0:T(8,128)(2,1)S(1)}, bf16[2,8,64,128]{3,2,1,0:T(8,128)(2,1)S(1)}, u32[]{:S(2)}, u32[]{:S(2)}) collective-permute-start(bf16[2,8,64,128]{3,2,1,0:T(8,128)(2,1)S(1)} %pad_maximum_fusion.2.refs_0_), channel_id=1, source_target_pairs={{0,4},{4,0},{8,12},{12,8},{16,20},{20,16},{24,28},{28,24},{1,5},{5... | collective-permute-start | bytes 786440 | tf_op jit(solution)/shard_map/ppermute | solution.py:28
  26.4 3.1 %collective-permute-start.6 = (bf16[2,8,64,128]{3,2,1,0:T(8,128)(2,1)S(1)}, bf16[2,8,64,128]{3,2,1,0:T(8,128)(2,1)S(1)}, u32[]{:S(2)}, u32[]{:S(2)}) collective-permute-start(bf16[2,8,64,128]{3,2,1,0:T(8,128)(2,1)S(1)} %collective-permute-done.2.refs_3_), channel_id=1, source_target_pairs={{0,4},{4,0},{8,12},{12,8},{16,20},{20,16},{24,28},{28,24},{1,5},{5... | collective-permute-start | bytes 786440 | tf_op jit(solution)/shard_map/ppermute | solution.py:28
  28.3 1.5 %collective-permute-start.5 = (bf16[2,8,64,128]{3,2,1,0:T(8,128)(2,1)S(1)}, bf16[2,8,64,128]{3,2,1,0:T(8,128)(2,1)S(1)}, u32[]{:S(2)}, u32[]{:S(2)}) collective-permute-start(bf16[2,8,64,128]{3,2,1,0:T(8,128)(2,1)S(1)} %collective-permute-done.1.refs_2_), channel_id=1, source_target_pairs={{0,4},{4,0},{8,12},{12,8},{16,20},{20,16},{24,28},{28,24},{1,5},{5... | collective-permute-start | bytes 786440 | tf_op jit(solution)/shard_map/ppermute | solution.py:28
  28.4 1.8 %collective-permute-start.4 = (bf16[2,8,64,128]{3,2,1,0:T(8,128)(2,1)S(1)}, bf16[2,8,64,128]{3,2,1,0:T(8,128)(2,1)S(1)}, u32[]{:S(2)}, u32[]{:S(2)}) collective-permute-start(bf16[2,8,64,128]{3,2,1,0:T(8,128)(2,1)S(1)} %collective-permute-done.refs_1_), channel_id=1, source_target_pairs={{0,4},{4,0},{8,12},{12,8},{16,20},{20,16},{24,28},{28,24},{1,5},{5... | collective-permute-start | bytes 786440 | tf_op jit(solution)/shard_map/ppermute | solution.py:28
  46.8 3.3 %collective-permute-start.16 = (bf16[8,64,128]{2,1,0:T(8,128)(2,1)S(1)}, bf16[8,64,128]{2,1,0:T(8,128)(2,1)S(1)}, u32[]{:S(2)}, u32[]{:S(2)}) collective-permute-start(bf16[8,64,128]{2,1,0:T(8,128)(2,1)S(1)} %get-tuple-element.20), channel_id=1, source_target_pairs={{0,4},{4,0},{8,12},{12,8},{16,20},{20,16},{24,28},{28,24},{1,5},{5... | collective-permute-start | bytes 393224 | tf_op jit(solution)/shard_map/ppermute | solution.py:28
  47.0 3.8 %collective-permute-start.17 = (bf16[8,64,128]{2,1,0:T(8,128)(2,1)S(1)}, bf16[8,64,128]{2,1,0:T(8,128)(2,1)S(1)}, u32[]{:S(2)}, u32[]{:S(2)}) collective-permute-start(bf16[8,64,128]{2,1,0:T(8,128)(2,1)S(1)} %get-tuple-element.22), channel_id=1, source_target_pairs={{0,4},{4,0},{8,12},{12,8},{16,20},{20,16},{24,28},{28,24},{1,5},{5... | collective-permute-start | bytes 393224 | tf_op jit(solution)/shard_map/ppermute | solution.py:28
  47.3 5.2 %collective-permute-start.19 = (bf16[8,64,128]{2,1,0:T(8,128)(2,1)S(1)}, bf16[8,64,128]{2,1,0:T(8,128)(2,1)S(1)}, u32[]{:S(2)}, u32[]{:S(2)}) collective-permute-start(bf16[8,64,128]{2,1,0:T(8,128)(2,1)S(1)} %get-tuple-element.24), channel_id=1, source_target_pairs={{0,4},{4,0},{8,12},{12,8},{16,20},{20,16},{24,28},{28,24},{1,5},{5... | collective-permute-start | bytes 393224 | tf_op jit(solution)/shard_map/ppermute | solution.py:28
  47.5 5.6 %collective-permute-start.21 = (bf16[8,64,128]{2,1,0:T(8,128)(2,1)S(1)}, bf16[8,64,128]{2,1,0:T(8,128)(2,1)S(1)}, u32[]{:S(2)}, u32[]{:S(2)}) collective-permute-start(bf16[8,64,128]{2,1,0:T(8,128)(2,1)S(1)} %get-tuple-element.26), channel_id=1, source_target_pairs={{0,4},{4,0},{8,12},{12,8},{16,20},{20,16},{24,28},{28,24},{1,5},{5... | collective-permute-start | bytes 393224 | tf_op jit(solution)/shard_map/ppermute | solution.py:28
  47.9 6.8 %collective-permute-start.23 = (bf16[2,4,64,128]{3,2,1,0:T(8,128)(2,1)S(1)}, bf16[2,4,64,128]{3,2,1,0:T(8,128)(2,1)S(1)}, u32[]{:S(2)}, u32[]{:S(2)}) collective-permute-start(bf16[2,4,64,128]{3,2,1,0:T(8,128)(2,1)S(1)} %get-tuple-element.28), channel_id=1, source_target_pairs={{0,24},{4,28},{8,0},{12,4},{16,8},{20,12},{24,16},{28,20},{1,25},{... | collective-permute-start | bytes 393224 | tf_op jit(solution)/shard_map/ppermute | solution.py:23
  50.1 6.9 %collective-permute-start.24 = (bf16[2,4,64,128]{3,2,1,0:T(8,128)(2,1)S(1)}, bf16[2,4,64,128]{3,2,1,0:T(8,128)(2,1)S(1)}, u32[]{:S(2)}, u32[]{:S(2)}) collective-permute-start(bf16[2,4,64,128]{3,2,1,0:T(8,128)(2,1)S(1)} %get-tuple-element.30), channel_id=1, source_target_pairs={{0,24},{4,28},{8,0},{12,4},{16,8},{20,12},{24,16},{28,20},{1,25},{... | collective-permute-start | bytes 393224 | tf_op jit(solution)/shard_map/ppermute | solution.py:23
  50.8 9.0 %collective-permute-start.26 = (bf16[2,4,64,128]{3,2,1,0:T(8,128)(2,1)S(1)}, bf16[2,4,64,128]{3,2,1,0:T(8,128)(2,1)S(1)}, u32[]{:S(2)}, u32[]{:S(2)}) collective-permute-start(bf16[2,4,64,128]{3,2,1,0:T(8,128)(2,1)S(1)} %get-tuple-element.32), channel_id=1, source_target_pairs={{0,24},{4,28},{8,0},{12,4},{16,8},{20,12},{24,16},{28,20},{1,25},{... | collective-permute-start | bytes 393224 | tf_op jit(solution)/shard_map/ppermute | solution.py:23
  52.5 9.3 %collective-permute-start.28 = (bf16[2,4,64,128]{3,2,1,0:T(8,128)(2,1)S(1)}, bf16[2,4,64,128]{3,2,1,0:T(8,128)(2,1)S(1)}, u32[]{:S(2)}, u32[]{:S(2)}) collective-permute-start(bf16[2,4,64,128]{3,2,1,0:T(8,128)(2,1)S(1)} %get-tuple-element.34), channel_id=1, source_target_pairs={{0,24},{4,28},{8,0},{12,4},{16,8},{20,12},{24,16},{28,20},{1,25},{... | collective-permute-start | bytes 393224 | tf_op jit(solution)/shard_map/ppermute | solution.py:23
  53.1 10.3 %collective-permute-start.18 = (bf16[8,64,128]{2,1,0:T(8,128)(2,1)S(1)}, bf16[8,64,128]{2,1,0:T(8,128)(2,1)S(1)}, u32[]{:S(2)}, u32[]{:S(2)}) collective-permute-start(bf16[8,64,128]{2,1,0:T(8,128)(2,1)S(1)} %add_convert_fusion.6), channel_id=1, source_target_pairs={{0,1},{1,0},{2,3},{3,2},{4,5},{5,4},{6,7},{7,6},{8,9},{9,8},{10,11... | collective-permute-start | bytes 393224 | tf_op jit(solution)/shard_map/ppermute | solution.py:18
  54.7 10.2 %collective-permute-start.20 = (bf16[8,64,128]{2,1,0:T(8,128)(2,1)S(1)}, bf16[8,64,128]{2,1,0:T(8,128)(2,1)S(1)}, u32[]{:S(2)}, u32[]{:S(2)}) collective-permute-start(bf16[8,64,128]{2,1,0:T(8,128)(2,1)S(1)} %add_convert_fusion.5), channel_id=1, source_target_pairs={{0,2},{1,3},{2,0},{3,1},{4,6},{5,7},{6,4},{7,5},{8,10},{9,11},{10,... | collective-permute-start | bytes 393224 | tf_op jit(solution)/shard_map/ppermute | solution.py:18
  57.0 7.9 %collective-permute-start.22 = (bf16[8,64,128]{2,1,0:T(8,128)(2,1)S(1)}, bf16[8,64,128]{2,1,0:T(8,128)(2,1)S(1)}, u32[]{:S(2)}, u32[]{:S(2)}) collective-permute-start(bf16[8,64,128]{2,1,0:T(8,128)(2,1)S(1)} %add_convert_fusion.4), channel_id=1, source_target_pairs={{0,3},{1,2},{2,1},{3,0},{4,7},{5,6},{6,5},{7,4},{8,11},{9,10},{10,... | collective-permute-start | bytes 393224 | tf_op jit(solution)/shard_map/ppermute | solution.py:18
  59.8 6.7 %collective-permute-start.25 = (bf16[2,4,64,128]{3,2,1,0:T(8,128)(2,1)S(1)}, bf16[2,4,64,128]{3,2,1,0:T(8,128)(2,1)S(1)}, u32[]{:S(2)}, u32[]{:S(2)}) collective-permute-start(bf16[2,4,64,128]{3,2,1,0:T(8,128)(2,1)S(1)} %add_convert_fusion.2), channel_id=1, source_target_pairs={{0,1},{1,0},{2,3},{3,2},{4,5},{5,4},{6,7},{7,6},{8,9},{9,8},{10,11... | collective-permute-start | bytes 393224 | tf_op jit(solution)/shard_map/ppermute | solution.py:18
  61.8 7.8 %collective-permute-start.27 = (bf16[2,4,64,128]{3,2,1,0:T(8,128)(2,1)S(1)}, bf16[2,4,64,128]{3,2,1,0:T(8,128)(2,1)S(1)}, u32[]{:S(2)}, u32[]{:S(2)}) collective-permute-start(bf16[2,4,64,128]{3,2,1,0:T(8,128)(2,1)S(1)} %add_convert_fusion.1), channel_id=1, source_target_pairs={{0,2},{1,3},{2,0},{3,1},{4,6},{5,7},{6,4},{7,5},{8,10},{9,11},{10,... | collective-permute-start | bytes 393224 | tf_op jit(solution)/shard_map/ppermute | solution.py:18
  63.4 6.2 %collective-permute-start.29 = (bf16[2,4,64,128]{3,2,1,0:T(8,128)(2,1)S(1)}, bf16[2,4,64,128]{3,2,1,0:T(8,128)(2,1)S(1)}, u32[]{:S(2)}, u32[]{:S(2)}) collective-permute-start(bf16[2,4,64,128]{3,2,1,0:T(8,128)(2,1)S(1)} %add_convert_fusion), channel_id=1, source_target_pairs={{0,3},{1,2},{2,1},{3,0},{4,7},{5,6},{6,5},{7,4},{8,11},{9,10},{10,... | collective-permute-start | bytes 393224 | tf_op jit(solution)/shard_map/ppermute | solution.py:18
  (3 other events, 2.4 us)

commit v2 on v1

--- a/solution.py
+++ b/solution.py
@@ -41,10 +41,8 @@
 def dot(a, b, contract):
     return lax.dot_general(a, b, ((contract[0], contract[1]), ((), ())), preferred_element_type=jnp.float32)
 
-
 NT = ((1,), (1,))
 NN = ((1,), (0,))
-
 
 def grads_kernel(planes, far, group, n_pieces, *refs):
     refs = list(refs)
@@ -59,74 +57,88 @@
     own_o, other_o, own_lse, other_lse, own_start, other_start = take(6)
     dq_own, dq_other = take(n_pieces), take(n_pieces)
     dkv = [take(n_pieces) for _ in range(planes + 1)]
-    acc_kv, acc_dq, ds_ref = take(3)
-
-    rows, width = own_q[0].shape[2], own_q[0].shape[3]
+    (mask_ref,) = take(1)
+
+    kv_heads, rows, width = kv[0][0].shape[1:]
     keys = rows * n_pieces
     ctx = lax.axis_index("ctx")
     head = lax.axis_index("head")
     core = ctx & 1
-
-    acc_kv[...] = jnp.zeros_like(acc_kv)
-    acc_dq[...] = jnp.zeros_like(acc_dq)
-
-    def load_q(pieces, which):
-        return jnp.concatenate([pieces[p][which, g] for g in range(group) for p in range(n_pieces)], axis=0)
-
-    lane = lax.broadcasted_iota(jnp.int32, (1, group * keys), 1) % keys
-    in_block = ((lane // rows) ^ head) * rows + lane % rows
-
-    q_sets = []
-    for pieces, o_ref, lse_ref, start_ref in (
-        (own_q, own_o, own_lse, own_start),
-        (other_q, other_o, other_lse, other_start),
-    ):
-        q_rows, g_rows = load_q(pieces, 0), load_q(pieces, 1)
-        o_rows = o_ref[...].reshape(group * keys, width)
-        prod = g_rows.astype(jnp.float32) * o_rows.astype(jnp.float32)
-        high = prod.astype(jnp.bfloat16)
-        low = (prod - high.astype(jnp.float32)).astype(jnp.bfloat16)
+    tasks = [(0, plane) for plane in range(planes + 1)]
+    tasks += [(1, plane) for plane in range(planes) if 2 * plane + 1 <= far]
+
+    row = lax.broadcasted_iota(jnp.int32, (keys, 1), 0)
+    lane = lax.broadcasted_iota(jnp.int32, (1, keys), 1)
+    spot = lambda x: ((x // rows) ^ head) * rows + x % rows
+    for n, (which, plane) in enumerate(tasks):
+        start = (own_start, other_start)[which][...]
+        behind = 2 * plane if which == 0 else 2 * (plane + core)
+        k_pos = (ctx - behind) * keys + spot(row)
+        allowed = k_pos >= start
+        if which == 0 and plane == 0:
+            allowed = allowed & (k_pos <= ctx * keys + spot(lane))
+        mask_ref[n] = jnp.where(allowed, 1.0, 0.0)
+
+    def one_head(i, carry):
         ones = jnp.ones((8, width), jnp.bfloat16)
-        delta = (dot(ones, high, NT) + dot(ones, low, NT))[0:1]
-        q_sets.append((q_rows, g_rows, delta, lse_ref[0] * log2e, start_ref[...]))
-
-    def pair(which_q, plane):
-        q_rows, g_rows, delta, lse2, start = q_sets[which_q]
-        key_ctx = ctx - 2 * plane
-        for p in range(n_pieces):
-            k_rows, v_rows = kv[plane][p][0, 0], kv[plane][p][1, 0]
-            k_pos = key_ctx * keys + (head ^ p) * rows + lax.broadcasted_iota(jnp.int32, (rows, 1), 0)
-            scores = dot(k_rows, q_rows, NT)
-            d_weights = dot(v_rows, g_rows, NT)
-            t = jnp.tanh(scores * (score_scale / soft_cap))
-            weights = jnp.exp2(t * (soft_cap * log2e) - lse2)
-            allowed = k_pos >= start
-            if which_q == 0 and plane == 0:
-                allowed = allowed & (k_pos <= ctx * keys + in_block)
-            weights = jnp.where(allowed, weights, 0.0)
-            d_scores = weights * (d_weights - delta) * ((1.0 - t * t) * score_scale)
-            d_scores = d_scores.astype(jnp.bfloat16)
-            ds_ref[pl.ds(p * rows, rows)] = d_scores
-            span = pl.ds(p * rows, rows)
-            acc_kv[plane, 0, span] += dot(d_scores, q_rows, NN)
-            acc_kv[plane, 1, span] += dot(weights.astype(jnp.bfloat16), g_rows, NN)
-        k_all = jnp.concatenate([kv[plane][p][0, 0] for p in range(n_pieces)], axis=0)
-        acc_dq[which_q] += dot(k_all.T, ds_ref[...], NN)
-
-    for plane in range(planes + 1):
-        pair(0, plane)
-        reached = ((core == 0) & (2 * plane + 1 <= far)) | ((core == 1) & (plane >= 1))
-        pl.when(reached)(functools.partial(pair, 1, plane))
-
-    for which_q, outs in ((0, dq_own), (1, dq_other)):
-        full = acc_dq[which_q].T.reshape(group, n_pieces, rows, width)
-        for p in range(n_pieces):
-            outs[p][...] = full[:, p].astype(outs[p].dtype)
-    for plane in range(planes + 1):
-        for p in range(n_pieces):
-            span = pl.ds(p * rows, rows)
-            for which in range(2):
-                dkv[plane][p][which, 0] = acc_kv[plane, which, span].astype(dkv[plane][p].dtype)
+        q_sets = []
+        for pieces, o_ref, lse_ref in ((own_q, own_o, own_lse), (other_q, other_o, other_lse)):
+            per_head = []
+            for g in range(group):
+                h = i * group + g
+                q_rows = jnp.concatenate([piece[0, h] for piece in pieces], axis=0)
+                g_rows = jnp.concatenate([piece[1, h] for piece in pieces], axis=0)
+                prod = g_rows.astype(jnp.float32) * o_ref[h].astype(jnp.float32)
+                high = prod.astype(jnp.bfloat16)
+                low = (prod - high.astype(jnp.float32)).astype(jnp.bfloat16)
+                delta = (dot(ones, high, NT) + dot(ones, low, NT))[0:1]
+                per_head.append((q_rows, g_rows, delta, lse_ref[i, :, g * keys : (g + 1) * keys] * log2e))
+            q_sets.append(per_head)
+        k_all, v_all = [], []
+        for plane in range(planes + 1):
+            k_all.append(jnp.concatenate([piece[0, i] for piece in kv[plane]], axis=0))
+            v_all.append(jnp.concatenate([piece[1, i] for piece in kv[plane]], axis=0))
+        dk = [None] * (planes + 1)
+        dv = [None] * (planes + 1)
+        dq = [[None] * group, [None] * group]
+        add = lambda a, b: b if a is None else a + b
+        for n, (which, plane) in enumerate(tasks):
+            if which == 0:
+                k_rows, v_rows = k_all[plane], v_all[plane]
+            else:
+                k_rows = jnp.where(core == 0, k_all[plane], k_all[plane + 1])
+                v_rows = jnp.where(core == 0, v_all[plane], v_all[plane + 1])
+            k_turned = k_rows.T
+            dk_part = dv_part = None
+            for g in range(group):
+                q_rows, g_rows, delta, lse2 = q_sets[which][g]
+                t = jnp.tanh(dot(k_rows, q_rows, NT) * (score_scale / soft_cap))
+                weights = jnp.exp2(t * (soft_cap * log2e) - lse2) * mask_ref[n]
+                d_scores = (weights * (dot(v_rows, g_rows, NT) - delta)) * (1.0 - t * t)
+                d_scores = d_scores.astype(jnp.bfloat16)
+                dk_part = add(dk_part, dot(d_scores, q_rows, NN))
+                dv_part = add(dv_part, dot(weights.astype(jnp.bfloat16), g_rows, NN))
+                dq[which][g] = add(dq[which][g], dot(k_turned, d_scores, NN))
+            if which == 0:
+                dk[plane], dv[plane] = dk_part, dv_part
+            else:
+                for side in range(2):
+                    chosen = core == side
+                    dk[plane + side] = dk[plane + side] + jnp.where(chosen, dk_part, 0.0)
+                    dv[plane + side] = dv[plane + side] + jnp.where(chosen, dv_part, 0.0)
+        for which, outs in ((0, dq_own), (1, dq_other)):
+            for g in range(group):
+                full = (dq[which][g] * score_scale).T
+                for p in range(n_pieces):
+                    outs[p][i * group + g] = full[p * rows : (p + 1) * rows].astype(outs[p].dtype)
+        for plane in range(planes + 1):
+            for p in range(n_pieces):
+                span = slice(p * rows, (p + 1) * rows)
+                dkv[plane][p][0, i] = (dk[plane][span] * score_scale).astype(dkv[plane][p].dtype)
+                dkv[plane][p][1, i] = dv[plane][span].astype(dkv[plane][p].dtype)
+        return carry
+
+    lax.fori_loop(0, kv_heads, one_head, 0, unroll=min(2, kv_heads))
 
 
 def grads_call(planes, far, group, own_q, other_q, kv, o_pair, lse_pair, start_pair):
@@ -135,30 +147,22 @@
     kv_heads = heads // group
     keys = rows * n_pieces
     f32, bf16 = jnp.float32, jnp.bfloat16
-    q_spec = pl.BlockSpec((2, group, rows, width), lambda i: (0, i, 0, 0))
-    kv_spec = pl.BlockSpec((2, 1, rows, width), lambda i: (0, i, 0, 0))
-    o_spec = pl.BlockSpec((group, keys, width), lambda i: (i, 0, 0))
-    lse_spec = pl.BlockSpec((1, 1, group * keys), lambda i: (i, 0, 0))
-    start_spec = pl.BlockSpec((1, group * keys), lambda i: (0, 0))
-    dq_spec = pl.BlockSpec((group, rows, width), lambda i: (i, 0, 0))
     shape = jax.ShapeDtypeStruct
     dq_shape, kv_shape = (heads, rows, width), (2, kv_heads, rows, width)
-    pairs = kv_heads * 3 * planes * group
+    pairs = kv_heads * (2 * planes + 1) * group
+    n_in = (planes + 3) * n_pieces + 6
+    n_out = (planes + 3) * n_pieces
+    vmem = pl.BlockSpec(memory_space=pltpu.VMEM)
     outs = pl.pallas_call(
         functools.partial(grads_kernel, planes, far, group, n_pieces),
-        grid=(kv_heads,),
-        in_specs=[q_spec] * (2 * n_pieces) + [kv_spec] * ((planes + 1) * n_pieces) + [o_spec] * 2 + [lse_spec] * 2 + [start_spec] * 2,
-        out_specs=[dq_spec] * (2 * n_pieces) + [kv_spec] * ((planes + 1) * n_pieces),
+        in_specs=[vmem] * n_in,
+        out_specs=[vmem] * n_out,
         out_shape=[shape(dq_shape, f32)] * n_pieces
         + [shape(dq_shape, bf16)] * n_pieces
         + [shape(kv_shape, f32)] * n_pieces
         + [shape(kv_shape, bf16)] * (planes * n_pieces),
-        scratch_shapes=[
-            pltpu.VMEM((planes + 1, 2, keys, width), f32),
-            pltpu.VMEM((2, width, group * keys), f32),
-            pltpu.VMEM((keys, group * keys), bf16),
-        ],
-        compiler_params=pltpu.CompilerParams(dimension_semantics=("arbitrary",), vmem_limit_bytes=24 * 1024 * 1024),
+        scratch_shapes=[pltpu.VMEM((2 * planes + 1, keys, keys), f32)],
+        compiler_params=pltpu.CompilerParams(vmem_limit_bytes=32 * 1024 * 1024),
         cost_estimate=pl.CostEstimate(
             flops=pairs * 10 * keys * keys * width, bytes_accessed=8 * 1024 * 1024, transcendentals=pairs * 2 * keys * keys
         ),
@@ -210,7 +214,7 @@
         lane = jnp.arange(tok, dtype=jnp.int32)
         pos = block * tok + ((lane // rows) ^ head) * rows + lane % rows
         start = jnp.max(jnp.where(doc_ends[None, :] <= pos[:, None], doc_ends[None, :], 0), axis=1)
-        return jnp.tile(start, group)[None]
+        return start[None]
 
     dq_own, dq_other, dkv_own, dkv_far = grads_call(
         planes, far, group, q_own, q_other, kv,

time: 72.2 us -> 71.5 us (level)
  Pallas kernels: 16.6 us -> 7.47 us
  local copies, waits for them, and re-layouts: 7.7 us -> 14.1 us
  waiting for transfers between devices: 13 us -> 14.4 us
    pallas_call x1, Pallas kernels: 16.6 us -> 7.47 us  [grads_call(): pl.pallas_call(functools.partial(grads_kernel, planes, far, group, n_piec...]
    unnamed x33 -> x49, local copies, waits for them, and re-layouts: 5.55 us -> 12 us
    ppermute x8, waiting for transfers between devices: 7.86 us -> 9.94 us  [rotate_ctx(): lax.ppermute(value, 'ctx', [(i, (i + steps) % count) for i in range(count)])]
  transfers between devices with their start and end apart: 30 -> 30, of which waited for: 10 -> 9; matrix products, arithmetic and copies ran while one was open for 8% -> 8% of each run, Pallas kernels for 0% -> 0%
where the time goes in v2:
time: 71.5 us; the launch traced here: 71.1 us
  starting transfers between devices  30.7 us (43%)
  waiting for transfers between devices  14.4 us (20%)
  local copies, waits for them, and re-layouts  14.1 us (20%)
  Pallas kernels  7.47 us (10%)
  other arithmetic  3.22 us (5%)
  between operations  1.17 us (2%)
    ppermute x12, starting transfers between devices, swap_heads(): return lax.ppermute(value, 'head', [(i, i ^ step) for i in range(count)])  17.4 us
    unnamed x49, local copies, waits for them, and re-layouts  12 us
    ppermute x8, starting transfers between devices, rotate_ctx(): lax.ppermute(value, 'ctx', [(i, (i + steps) % count) for i in range(count)])  10.7 us
    ppermute x8, waiting for transfers between devices, rotate_ctx(): lax.ppermute(value, 'ctx', [(i, (i + steps) % count) for i in range(count)])  9.94 us
    pallas_call x1, Pallas kernels, grads_call(): pl.pallas_call(functools.partial(grads_kernel, planes, far, group, n_piec...  7.47 us
    ppermute x12, waiting for transfers between devices, swap_heads(): return lax.ppermute(value, 'head', [(i, i ^ step) for i in range(count)])  4.47 us
    ppermute x10, starting transfers between devices, swap_cores(): return lax.ppermute(value, 'ctx', [(i, i ^ 1) for i in range(count)])  2.6 us
  transfers between devices with their start and end apart: 30, of which 9 were waited for; matrix products, arithmetic and copies ran while one was open for 8% of the time, Pallas kernels for 0%

profile of v2, /device:TPU:0, one launch (start us, length us, event | category | flops | bytes accessed | tf_op | source)
XLA Modules:
  0.0 71.1 jit_solution(412786968366522323)
XLA Ops:
  2.2 1.2 %constant_dynamic-slice_fusion = (bf16[64,1,4,128]{3,2,1,0:T(4,128)(2,1)S(1)}, bf16[64,1,4,128]{3,2,1,0:T(4,128)(2,1)S(1)}, bf16[64,1,4,128]{3,2,1,0:T(4,128)(2,...) fusion(bf16[64,4,4,128]{3,2,1,0:T(4,128)(2,1)} %bitcast.231, ...), kind=kLoop, calls=%fused_computation.49 | loop fusion | bytes 1048592 | tf_op jit(solution)/shard_map/jit(dynamic_index_in_dim)/dynamic_slice | solution.py:188
  4.1 3.5 %collective-permute-start.9 = (bf16[2,4,64,128]{3,2,1,0:T(8,128)(2,1)}, bf16[2,4,64,128]{3,2,1,0:T(8,128)(2,1)S(1)}, u32[]{:S(2)}, u32[]{:S(2)}) collective-permute-start(bf16[2,4,64,128]{3,2,1,0:T(8,128)(2,1)} %pad_maximum_fusion.9), channel_id=1, source_target_pairs={{0,3},{1,2},{2,1},{3,0},{4,7},{5,6},{6,5},{7,4},{8,11},{9,10},{10,... | collective-permute-start | bytes 393224 | tf_op jit(solution)/shard_map/ppermute | solution.py:18
  8.5 2.1 %collective-permute-start.10 = (bf16[2,4,64,128]{3,2,1,0:T(8,128)(2,1)S(1)}, bf16[2,4,64,128]{3,2,1,0:T(8,128)(2,1)S(1)}, u32[]{:S(2)}, u32[]{:S(2)}) collective-permute-start(bf16[2,4,64,128]{3,2,1,0:T(8,128)(2,1)S(1)} %pad_maximum_fusion.6.refs_8_), channel_id=1, source_target_pairs={{0,8},{4,12},{8,16},{12,20},{16,24},{20,28},{24,0},{28,4},{1,9},{5... | collective-permute-start | bytes 393224 | tf_op jit(solution)/shard_map/ppermute | solution.py:23
  11.2 0.9 %copy-done.11 = bf16[64,32,128]{2,1,0:T(8,128)(2,1)S(1)} copy-done((bf16[64,32,128]{2,1,0:T(8,128)(2,1)S(1)}, bf16[64,32,128]{2,1,0:T(8,128)(2,1)}, u32[]{:S(2)}) %copy-start.11) | copy-done | bytes 524312
  12.6 1.6 %collective-permute-start.13 = (bf16[2,4,64,128]{3,2,1,0:T(8,128)(2,1)S(1)}, bf16[2,4,64,128]{3,2,1,0:T(8,128)(2,1)S(1)}, u32[]{:S(2)}, u32[]{:S(2)}) collective-permute-start(bf16[2,4,64,128]{3,2,1,0:T(8,128)(2,1)S(1)} %collective-permute-done.9.refs_11_), channel_id=1, source_target_pairs={{0,8},{4,12},{8,16},{12,20},{16,24},{20,28},{24,0},{28,4},{1,9},{5... | collective-permute-start | bytes 393224 | tf_op jit(solution)/shard_map/ppermute | solution.py:23
  14.7 1.8 %collective-permute-start.12 = (bf16[2,4,64,128]{3,2,1,0:T(8,128)(2,1)S(1)}, bf16[2,4,64,128]{3,2,1,0:T(8,128)(2,1)S(1)}, u32[]{:S(2)}, u32[]{:S(2)}) collective-permute-start(bf16[2,4,64,128]{3,2,1,0:T(8,128)(2,1)S(1)} %collective-permute-done.8.refs_10_), channel_id=1, source_target_pairs={{0,8},{4,12},{8,16},{12,20},{16,24},{20,28},{24,0},{28,4},{1,9},{5... | collective-permute-start | bytes 393224 | tf_op jit(solution)/shard_map/ppermute | solution.py:23
  16.5 2.0 %collective-permute-start.2 = (bf16[2,8,64,128]{3,2,1,0:T(8,128)(2,1)S(1)}, bf16[2,8,64,128]{3,2,1,0:T(8,128)(2,1)S(1)}, u32[]{:S(2)}, u32[]{:S(2)}) collective-permute-start(bf16[2,8,64,128]{3,2,1,0:T(8,128)(2,1)S(1)} %pad_maximum_fusion.5), channel_id=1, source_target_pairs={{0,3},{1,2},{2,1},{3,0},{4,7},{5,6},{6,5},{7,4},{8,11},{9,10},{10,... | collective-permute-start | bytes 786440 | tf_op jit(solution)/shard_map/ppermute | solution.py:18
  18.6 1.0 %collective-permute-start.1 = (bf16[2,8,64,128]{3,2,1,0:T(8,128)(2,1)S(1)}, bf16[2,8,64,128]{3,2,1,0:T(8,128)(2,1)S(1)}, u32[]{:S(2)}, u32[]{:S(2)}) collective-permute-start(bf16[2,8,64,128]{3,2,1,0:T(8,128)(2,1)S(1)} %pad_maximum_fusion.4), channel_id=1, source_target_pairs={{0,2},{1,3},{2,0},{3,1},{4,6},{5,7},{6,4},{7,5},{8,10},{9,11},{10,... | collective-permute-start | bytes 786440 | tf_op jit(solution)/shard_map/ppermute | solution.py:18
  20.2 1.4 %collective-permute-start = (bf16[2,8,64,128]{3,2,1,0:T(8,128)(2,1)S(1)}, bf16[2,8,64,128]{3,2,1,0:T(8,128)(2,1)S(1)}, u32[]{:S(2)}, u32[]{:S(2)}) collective-permute-start(bf16[2,8,64,128]{3,2,1,0:T(8,128)(2,1)S(1)} %pad_maximum_fusion.3), channel_id=1, source_target_pairs={{0,1},{1,0},{2,3},{3,2},{4,5},{5,4},{6,7},{7,6},{8,9},{9,8},{10,11... | collective-permute-start | bytes 786440 | tf_op jit(solution)/shard_map/ppermute | solution.py:18
  23.1 6.6 %collective-permute-done.11.refs_13_ = bf16[2,4,64,128]{3,2,1,0:T(8,128)(2,1)S(1)} collective-permute-done((bf16[2,4,64,128]{3,2,1,0:T(8,128)(2,1)S(1)}, bf16[2,4,64,128]{3,2,1,0:T(8,128)(2,1)S(1)}, u32[]{:S(2)}, u32[]{:S(2)}) %collective-permute-start.11) | collective-permute-done | bytes 131104 | tf_op jit(solution)/shard_map/ppermute | solution.py:23
  30.8 0.9 %collective-permute-done.1.refs_2_ = bf16[2,8,64,128]{3,2,1,0:T(8,128)(2,1)S(1)} collective-permute-done((bf16[2,8,64,128]{3,2,1,0:T(8,128)(2,1)S(1)}, bf16[2,8,64,128]{3,2,1,0:T(8,128)(2,1)S(1)}, u32[]{:S(2)}, u32[]{:S(2)}) %collective-permute-start.1) | collective-permute-done | bytes 262176 | tf_op jit(solution)/shard_map/ppermute | solution.py:18
  33.2 0.7 convert_element_type.55.refs_19_
  34.0 0.9 %copy-done.1 = bf16[2,4,64,128]{3,2,1,0:T(8,128)(2,1)S(1)} copy-done((bf16[2,4,64,128]{3,2,1,0:T(8,128)(2,1)S(1)}, bf16[2,4,64,128]{3,2,1,0:T(8,128)(2,1)}, u32[]{:S(2)}) %copy-start.1) | copy-done | bytes 131096
  34.9 0.9 %copy-done.3 = bf16[2,4,64,128]{3,2,1,0:T(8,128)(2,1)S(1)} copy-done((bf16[2,4,64,128]{3,2,1,0:T(8,128)(2,1)S(1)}, bf16[2,4,64,128]{3,2,1,0:T(8,128)(2,1)}, u32[]{:S(2)}) %copy-start.3) | copy-done | bytes 131096
  35.8 0.9 %copy-done.5 = bf16[2,4,64,128]{3,2,1,0:T(8,128)(2,1)S(1)} copy-done((bf16[2,4,64,128]{3,2,1,0:T(8,128)(2,1)S(1)}, bf16[2,4,64,128]{3,2,1,0:T(8,128)(2,1)}, u32[]{:S(2)}) %copy-start.5) | copy-done | bytes 131096
  36.7 0.9 %copy-done.7 = bf16[2,4,64,128]{3,2,1,0:T(8,128)(2,1)S(1)} copy-done((bf16[2,4,64,128]{3,2,1,0:T(8,128)(2,1)S(1)}, bf16[2,4,64,128]{3,2,1,0:T(8,128)(2,1)}, u32[]{:S(2)}) %copy-start.7) | copy-done | bytes 131096
  37.6 0.9 %copy-done.9 = bf16[2,4,64,128]{3,2,1,0:T(8,128)(2,1)S(1)} copy-done((bf16[2,4,64,128]{3,2,1,0:T(8,128)(2,1)S(1)}, bf16[2,4,64,128]{3,2,1,0:T(8,128)(2,1)}, u32[]{:S(2)}) %copy-start.9) | copy-done | bytes 131096
  38.5 7.5 %grads.1 = (f32[8,64,128]{2,1,0:T(8,128)S(1)}, f32[8,64,128]{2,1,0:T(8,128)S(1)}, f32[8,64,128]{2,1,0:T(8,128)S(1)}, f32[8,64,128]{2,1,0:T(8,128)S(1)}, bf16[8,6...) custom-call(bf16[2,8,64,128]{3,2,1,0:T(8,128)(2,1)S(1)} %pad_maximum, ...), custom_call_target="tpu_custom_call" | custom-call | flops 2013265920 | bytes 8388608 | tf_op jit(solution)/shard_map/grads/pallas_call | solution.py:156
  47.1 2.0 %collective-permute-start.23 = (bf16[2,4,64,128]{3,2,1,0:T(8,128)(2,1)S(1)}, bf16[2,4,64,128]{3,2,1,0:T(8,128)(2,1)S(1)}, u32[]{:S(2)}, u32[]{:S(2)}) collective-permute-start(bf16[2,4,64,128]{3,2,1,0:T(8,128)(2,1)S(1)} %get-tuple-element.28), channel_id=1, source_target_pairs={{0,24},{4,28},{8,0},{12,4},{16,8},{20,12},{24,16},{28,20},{1,25},{... | collective-permute-start | bytes 393224 | tf_op jit(solution)/shard_map/ppermute | solution.py:23
  49.1 2.0 %collective-permute-start.24 = (bf16[2,4,64,128]{3,2,1,0:T(8,128)(2,1)S(1)}, bf16[2,4,64,128]{3,2,1,0:T(8,128)(2,1)S(1)}, u32[]{:S(2)}, u32[]{:S(2)}) collective-permute-start(bf16[2,4,64,128]{3,2,1,0:T(8,128)(2,1)S(1)} %get-tuple-element.30), channel_id=1, source_target_pairs={{0,24},{4,28},{8,0},{12,4},{16,8},{20,12},{24,16},{28,20},{1,25},{... | collective-permute-start | bytes 393224 | tf_op jit(solution)/shard_map/ppermute | solution.py:23
  52.3 1.6 %collective-permute-start.18 = (bf16[8,64,128]{2,1,0:T(8,128)(2,1)S(1)}, bf16[8,64,128]{2,1,0:T(8,128)(2,1)S(1)}, u32[]{:S(2)}, u32[]{:S(2)}) collective-permute-start(bf16[8,64,128]{2,1,0:T(8,128)(2,1)S(1)} %add_convert_fusion.6), channel_id=1, source_target_pairs={{0,1},{1,0},{2,3},{3,2},{4,5},{5,4},{6,7},{7,6},{8,9},{9,8},{10,11... | collective-permute-start | bytes 393224 | tf_op jit(solution)/shard_map/ppermute | solution.py:18
  53.9 1.0 %collective-permute-start.20 = (bf16[8,64,128]{2,1,0:T(8,128)(2,1)S(1)}, bf16[8,64,128]{2,1,0:T(8,128)(2,1)S(1)}, u32[]{:S(2)}, u32[]{:S(2)}) collective-permute-start(bf16[8,64,128]{2,1,0:T(8,128)(2,1)S(1)} %add_convert_fusion.5), channel_id=1, source_target_pairs={{0,2},{1,3},{2,0},{3,1},{4,6},{5,7},{6,4},{7,5},{8,10},{9,11},{10,... | collective-permute-start | bytes 393224 | tf_op jit(solution)/shard_map/ppermute | solution.py:18
  54.9 1.3 %collective-permute-done.24 = bf16[2,4,64,128]{3,2,1,0:T(8,128)(2,1)S(1)} collective-permute-done((bf16[2,4,64,128]{3,2,1,0:T(8,128)(2,1)S(1)}, bf16[2,4,64,128]{3,2,1,0:T(8,128)(2,1)S(1)}, u32[]{:S(2)}, u32[]{:S(2)}) %collective-permute-start.24) | collective-permute-done | bytes 131104 | tf_op jit(solution)/shard_map/ppermute | solution.py:23
  56.2 1.8 %collective-permute-start.22 = (bf16[8,64,128]{2,1,0:T(8,128)(2,1)S(1)}, bf16[8,64,128]{2,1,0:T(8,128)(2,1)S(1)}, u32[]{:S(2)}, u32[]{:S(2)}) collective-permute-start(bf16[8,64,128]{2,1,0:T(8,128)(2,1)S(1)} %add_convert_fusion.4), channel_id=1, source_target_pairs={{0,3},{1,2},{2,1},{3,0},{4,7},{5,6},{6,5},{7,4},{8,11},{9,10},{10,... | collective-permute-start | bytes 393224 | tf_op jit(solution)/shard_map/ppermute | solution.py:18
  58.0 1.0 %collective-permute-done.26 = bf16[2,4,64,128]{3,2,1,0:T(8,128)(2,1)S(1)} collective-permute-done((bf16[2,4,64,128]{3,2,1,0:T(8,128)(2,1)S(1)}, bf16[2,4,64,128]{3,2,1,0:T(8,128)(2,1)S(1)}, u32[]{:S(2)}, u32[]{:S(2)}) %collective-permute-start.26) | collective-permute-done | bytes 131104 | tf_op jit(solution)/shard_map/ppermute | solution.py:23
  59.0 1.5 %collective-permute-start.25 = (bf16[2,4,64,128]{3,2,1,0:T(8,128)(2,1)S(1)}, bf16[2,4,64,128]{3,2,1,0:T(8,128)(2,1)S(1)}, u32[]{:S(2)}, u32[]{:S(2)}) collective-permute-start(bf16[2,4,64,128]{3,2,1,0:T(8,128)(2,1)S(1)} %add_convert_fusion.2), channel_id=1, source_target_pairs={{0,1},{1,0},{2,3},{3,2},{4,5},{5,4},{6,7},{7,6},{8,9},{9,8},{10,11... | collective-permute-start | bytes 393224 | tf_op jit(solution)/shard_map/ppermute | solution.py:18
  61.0 1.5 %collective-permute-start.27 = (bf16[2,4,64,128]{3,2,1,0:T(8,128)(2,1)S(1)}, bf16[2,4,64,128]{3,2,1,0:T(8,128)(2,1)S(1)}, u32[]{:S(2)}, u32[]{:S(2)}) collective-permute-start(bf16[2,4,64,128]{3,2,1,0:T(8,128)(2,1)S(1)} %add_convert_fusion.1), channel_id=1, source_target_pairs={{0,2},{1,3},{2,0},{3,1},{4,6},{5,7},{6,4},{7,5},{8,10},{9,11},{10,... | collective-permute-start | bytes 393224 | tf_op jit(solution)/shard_map/ppermute | solution.py:18
  62.5 1.5 %collective-permute-start.29 = (bf16[2,4,64,128]{3,2,1,0:T(8,128)(2,1)S(1)}, bf16[2,4,64,128]{3,2,1,0:T(8,128)(2,1)S(1)}, u32[]{:S(2)}, u32[]{:S(2)}) collective-permute-start(bf16[2,4,64,128]{3,2,1,0:T(8,128)(2,1)S(1)} %add_convert_fusion), channel_id=1, source_target_pairs={{0,3},{1,2},{2,1},{3,0},{4,7},{5,6},{6,5},{7,4},{8,11},{9,10},{10,... | collective-permute-start | bytes 393224 | tf_op jit(solution)/shard_map/ppermute | solution.py:18
  64.6 1.1 %copy.101 = bf16[64,32,128]{2,1,0:T(8,128)(2,1)} copy(bf16[64,32,128]{2,0,1:T(8,128)(2,1)S(1)} %bitcast.196) | data formatting | bytes 1048576
  65.7 3.1 %collective-permute-done.27 = bf16[2,4,64,128]{3,2,1,0:T(8,128)(2,1)S(1)} collective-permute-done((bf16[2,4,64,128]{3,2,1,0:T(8,128)(2,1)S(1)}, bf16[2,4,64,128]{3,2,1,0:T(8,128)(2,1)S(1)}, u32[]{:S(2)}, u32[]{:S(2)}) %collective-permute-start.27) | collective-permute-done | bytes 131104 | tf_op jit(solution)/shard_map/ppermute | solution.py:18
  69.3 0.9 %copy.103 = bf16[64,16,128]{2,1,0:T(8,128)(2,1)} copy(bf16[64,16,128]{2,0,1:T(8,128)(2,1)S(1)} %bitcast.200) | data formatting | bytes 524288
  70.2 0.9 %copy.102 = bf16[64,16,128]{2,1,0:T(8,128)(2,1)} copy(bf16[64,16,128]{2,0,1:T(8,128)(2,1)S(1)} %bitcast.199) | data formatting | bytes 524288
  (125 shorter events, 13.1 us)
Async XLA Ops:
  1.6 14.9 %collective-permute-start.15 = (bf16[4,1,512]{2,1,0:T(2,128)(2,1)S(1)}, bf16[4,1,512]{2,1,0:T(2,128)(2,1)}, u32[]{:S(2)}, u32[]{:S(2)}) collective-permute-start(bf16[4,1,512]{2,1,0:T(2,128)(2,1)S(1)} %copy.99), channel_id=1, source_target_pairs={{0,4},{4,0},{8,12},{12,8},{16,20},{20,16},{24,28},{28,24},{1,5},{5... | collective-permute-start | bytes 12296 | tf_op jit(solution)/shard_map/ppermute | solution.py:28
  4.1 8.5 %collective-permute-start.9 = (bf16[2,4,64,128]{3,2,1,0:T(8,128)(2,1)}, bf16[2,4,64,128]{3,2,1,0:T(8,128)(2,1)S(1)}, u32[]{:S(2)}, u32[]{:S(2)}) collective-permute-start(bf16[2,4,64,128]{3,2,1,0:T(8,128)(2,1)} %pad_maximum_fusion.9), channel_id=1, source_target_pairs={{0,3},{1,2},{2,1},{3,0},{4,7},{5,6},{6,5},{7,4},{8,11},{9,10},{10,... | collective-permute-start | bytes 393224 | tf_op jit(solution)/shard_map/ppermute | solution.py:18
  7.7 7.1 %collective-permute-start.8 = (bf16[2,4,64,128]{3,2,1,0:T(8,128)(2,1)S(1)}, bf16[2,4,64,128]{3,2,1,0:T(8,128)(2,1)S(1)}, u32[]{:S(2)}, u32[]{:S(2)}) collective-permute-start(bf16[2,4,64,128]{3,2,1,0:T(8,128)(2,1)S(1)} %pad_maximum_fusion.8), channel_id=1, source_target_pairs={{0,2},{1,3},{2,0},{3,1},{4,6},{5,7},{6,4},{7,5},{8,10},{9,11},{10,... | collective-permute-start | bytes 393224 | tf_op jit(solution)/shard_map/ppermute | solution.py:18
  8.3 8.2 %collective-permute-start.7 = (bf16[2,4,64,128]{3,2,1,0:T(8,128)(2,1)S(1)}, bf16[2,4,64,128]{3,2,1,0:T(8,128)(2,1)S(1)}, u32[]{:S(2)}, u32[]{:S(2)}) collective-permute-start(bf16[2,4,64,128]{3,2,1,0:T(8,128)(2,1)S(1)} %pad_maximum_fusion.7), channel_id=1, source_target_pairs={{0,1},{1,0},{2,3},{3,2},{4,5},{5,4},{6,7},{7,6},{8,9},{9,8},{10,11... | collective-permute-start | bytes 393224 | tf_op jit(solution)/shard_map/ppermute | solution.py:18
  8.5 10.1 %collective-permute-start.10 = (bf16[2,4,64,128]{3,2,1,0:T(8,128)(2,1)S(1)}, bf16[2,4,64,128]{3,2,1,0:T(8,128)(2,1)S(1)}, u32[]{:S(2)}, u32[]{:S(2)}) collective-permute-start(bf16[2,4,64,128]{3,2,1,0:T(8,128)(2,1)S(1)} %pad_maximum_fusion.6.refs_8_), channel_id=1, source_target_pairs={{0,8},{4,12},{8,16},{12,20},{16,24},{20,28},{24,0},{28,4},{1,9},{5... | collective-permute-start | bytes 393224 | tf_op jit(solution)/shard_map/ppermute | solution.py:23
  12.6 7.0 %collective-permute-start.13 = (bf16[2,4,64,128]{3,2,1,0:T(8,128)(2,1)S(1)}, bf16[2,4,64,128]{3,2,1,0:T(8,128)(2,1)S(1)}, u32[]{:S(2)}, u32[]{:S(2)}) collective-permute-start(bf16[2,4,64,128]{3,2,1,0:T(8,128)(2,1)S(1)} %collective-permute-done.9.refs_11_), channel_id=1, source_target_pairs={{0,8},{4,12},{8,16},{12,20},{16,24},{20,28},{24,0},{28,4},{1,9},{5... | collective-permute-start | bytes 393224 | tf_op jit(solution)/shard_map/ppermute | solution.py:23
  14.7 7.5 %collective-permute-start.12 = (bf16[2,4,64,128]{3,2,1,0:T(8,128)(2,1)S(1)}, bf16[2,4,64,128]{3,2,1,0:T(8,128)(2,1)S(1)}, u32[]{:S(2)}, u32[]{:S(2)}) collective-permute-start(bf16[2,4,64,128]{3,2,1,0:T(8,128)(2,1)S(1)} %collective-permute-done.8.refs_10_), channel_id=1, source_target_pairs={{0,8},{4,12},{8,16},{12,20},{16,24},{20,28},{24,0},{28,4},{1,9},{5... | collective-permute-start | bytes 393224 | tf_op jit(solution)/shard_map/ppermute | solution.py:23
  16.5 17.4 %collective-permute-start.14 = (bf16[8,256,128]{2,1,0:T(8,128)(2,1)S(1)}, bf16[8,256,128]{2,1,0:T(8,128)(2,1)S(1)}, u32[]{:S(2)}, u32[]{:S(2)}) collective-permute-start(bf16[8,256,128]{2,1,0:T(8,128)(2,1)S(1)} %bitcast.182), channel_id=1, source_target_pairs={{0,4},{4,0},{8,12},{12,8},{16,20},{20,16},{24,28},{28,24},{1,5},{5... | collective-permute-start | bytes 1572872 | tf_op jit(solution)/shard_map/ppermute | solution.py:28
  16.5 6.5 %copy-start = (bf16[2,4,64,128]{3,2,1,0:T(8,128)(2,1)}, bf16[2,4,64,128]{3,2,1,0:T(8,128)(2,1)S(1)}, u32[]{:S(2)}) copy-start(bf16[2,4,64,128]{3,2,1,0:T(8,128)(2,1)S(1)} %collective-permute-done.7.refs_9_) | copy-start | bytes 393220
  16.5 13.8 %collective-permute-start.2 = (bf16[2,8,64,128]{3,2,1,0:T(8,128)(2,1)S(1)}, bf16[2,8,64,128]{3,2,1,0:T(8,128)(2,1)S(1)}, u32[]{:S(2)}, u32[]{:S(2)}) collective-permute-start(bf16[2,8,64,128]{3,2,1,0:T(8,128)(2,1)S(1)} %pad_maximum_fusion.5), channel_id=1, source_target_pairs={{0,3},{1,2},{2,1},{3,0},{4,7},{5,6},{6,5},{7,4},{8,11},{9,10},{10,... | collective-permute-start | bytes 786440 | tf_op jit(solution)/shard_map/ppermute | solution.py:18
  18.5 4.5 %copy-start.2 = (bf16[2,4,64,128]{3,2,1,0:T(8,128)(2,1)}, bf16[2,4,64,128]{3,2,1,0:T(8,128)(2,1)S(1)}, u32[]{:S(2)}) copy-start(bf16[2,4,64,128]{3,2,1,0:T(8,128)(2,1)S(1)} %collective-permute-done.10.refs_12_) | copy-start | bytes 393220
  18.6 13.2 %collective-permute-start.1 = (bf16[2,8,64,128]{3,2,1,0:T(8,128)(2,1)S(1)}, bf16[2,8,64,128]{3,2,1,0:T(8,128)(2,1)S(1)}, u32[]{:S(2)}, u32[]{:S(2)}) collective-permute-start(bf16[2,8,64,128]{3,2,1,0:T(8,128)(2,1)S(1)} %pad_maximum_fusion.4), channel_id=1, source_target_pairs={{0,2},{1,3},{2,0},{3,1},{4,6},{5,7},{6,4},{7,5},{8,10},{9,11},{10,... | collective-permute-start | bytes 786440 | tf_op jit(solution)/shard_map/ppermute | solution.py:18
  20.2 11.6 %collective-permute-start = (bf16[2,8,64,128]{3,2,1,0:T(8,128)(2,1)S(1)}, bf16[2,8,64,128]{3,2,1,0:T(8,128)(2,1)S(1)}, u32[]{:S(2)}, u32[]{:S(2)}) collective-permute-start(bf16[2,8,64,128]{3,2,1,0:T(8,128)(2,1)S(1)} %pad_maximum_fusion.3), channel_id=1, source_target_pairs={{0,1},{1,0},{2,3},{3,2},{4,5},{5,4},{6,7},{7,6},{8,9},{9,8},{10,11... | collective-permute-start | bytes 786440 | tf_op jit(solution)/shard_map/ppermute | solution.py:18
  22.9 6.8 %collective-permute-start.11 = (bf16[2,4,64,128]{3,2,1,0:T(8,128)(2,1)S(1)}, bf16[2,4,64,128]{3,2,1,0:T(8,128)(2,1)S(1)}, u32[]{:S(2)}, u32[]{:S(2)}) collective-permute-start(bf16[2,4,64,128]{3,2,1,0:T(8,128)(2,1)S(1)} %collective-permute-done.7.refs_9_), channel_id=1, source_target_pairs={{0,8},{4,12},{8,16},{12,20},{16,24},{20,28},{24,0},{28,4},{1,9},{5... | collective-permute-start | bytes 393224 | tf_op jit(solution)/shard_map/ppermute | solution.py:23
  30.3 3.6 %collective-permute-start.3 = (bf16[2,8,64,128]{3,2,1,0:T(8,128)(2,1)S(1)}, bf16[2,8,64,128]{3,2,1,0:T(8,128)(2,1)S(1)}, u32[]{:S(2)}, u32[]{:S(2)}) collective-permute-start(bf16[2,8,64,128]{3,2,1,0:T(8,128)(2,1)S(1)} %pad_maximum_fusion.2.refs_0_), channel_id=1, source_target_pairs={{0,4},{4,0},{8,12},{12,8},{16,20},{20,16},{24,28},{28,24},{1,5},{5... | collective-permute-start | bytes 786440 | tf_op jit(solution)/shard_map/ppermute | solution.py:28
  30.3 3.6 %collective-permute-start.6 = (bf16[2,8,64,128]{3,2,1,0:T(8,128)(2,1)S(1)}, bf16[2,8,64,128]{3,2,1,0:T(8,128)(2,1)S(1)}, u32[]{:S(2)}, u32[]{:S(2)}) collective-permute-start(bf16[2,8,64,128]{3,2,1,0:T(8,128)(2,1)S(1)} %collective-permute-done.2.refs_3_), channel_id=1, source_target_pairs={{0,4},{4,0},{8,12},{12,8},{16,20},{20,16},{24,28},{28,24},{1,5},{5... | collective-permute-start | bytes 786440 | tf_op jit(solution)/shard_map/ppermute | solution.py:28
  31.8 2.2 %collective-permute-start.5 = (bf16[2,8,64,128]{3,2,1,0:T(8,128)(2,1)S(1)}, bf16[2,8,64,128]{3,2,1,0:T(8,128)(2,1)S(1)}, u32[]{:S(2)}, u32[]{:S(2)}) collective-permute-start(bf16[2,8,64,128]{3,2,1,0:T(8,128)(2,1)S(1)} %collective-permute-done.1.refs_2_), channel_id=1, source_target_pairs={{0,4},{4,0},{8,12},{12,8},{16,20},{20,16},{24,28},{28,24},{1,5},{5... | collective-permute-start | bytes 786440 | tf_op jit(solution)/shard_map/ppermute | solution.py:28
  31.9 2.1 %collective-permute-start.4 = (bf16[2,8,64,128]{3,2,1,0:T(8,128)(2,1)S(1)}, bf16[2,8,64,128]{3,2,1,0:T(8,128)(2,1)S(1)}, u32[]{:S(2)}, u32[]{:S(2)}) collective-permute-start(bf16[2,8,64,128]{3,2,1,0:T(8,128)(2,1)S(1)} %collective-permute-done.refs_1_), channel_id=1, source_target_pairs={{0,4},{4,0},{8,12},{12,8},{16,20},{20,16},{24,28},{28,24},{1,5},{5... | collective-permute-start | bytes 786440 | tf_op jit(solution)/shard_map/ppermute | solution.py:28
  46.0 3.1 %collective-permute-start.16 = (bf16[8,64,128]{2,1,0:T(8,128)(2,1)S(1)}, bf16[8,64,128]{2,1,0:T(8,128)(2,1)S(1)}, u32[]{:S(2)}, u32[]{:S(2)}) collective-permute-start(bf16[8,64,128]{2,1,0:T(8,128)(2,1)S(1)} %get-tuple-element.20), channel_id=1, source_target_pairs={{0,4},{4,0},{8,12},{12,8},{16,20},{20,16},{24,28},{28,24},{1,5},{5... | collective-permute-start | bytes 393224 | tf_op jit(solution)/shard_map/ppermute | solution.py:28
  46.1 5.0 %collective-permute-start.17 = (bf16[8,64,128]{2,1,0:T(8,128)(2,1)S(1)}, bf16[8,64,128]{2,1,0:T(8,128)(2,1)S(1)}, u32[]{:S(2)}, u32[]{:S(2)}) collective-permute-start(bf16[8,64,128]{2,1,0:T(8,128)(2,1)S(1)} %get-tuple-element.22), channel_id=1, source_target_pairs={{0,4},{4,0},{8,12},{12,8},{16,20},{20,16},{24,28},{28,24},{1,5},{5... | collective-permute-start | bytes 393224 | tf_op jit(solution)/shard_map/ppermute | solution.py:28
  46.5 5.2 %collective-permute-start.19 = (bf16[8,64,128]{2,1,0:T(8,128)(2,1)S(1)}, bf16[8,64,128]{2,1,0:T(8,128)(2,1)S(1)}, u32[]{:S(2)}, u32[]{:S(2)}) collective-permute-start(bf16[8,64,128]{2,1,0:T(8,128)(2,1)S(1)} %get-tuple-element.24), channel_id=1, source_target_pairs={{0,4},{4,0},{8,12},{12,8},{16,20},{20,16},{24,28},{28,24},{1,5},{5... | collective-permute-start | bytes 393224 | tf_op jit(solution)/shard_map/ppermute | solution.py:28
  46.6 5.6 %collective-permute-start.21 = (bf16[8,64,128]{2,1,0:T(8,128)(2,1)S(1)}, bf16[8,64,128]{2,1,0:T(8,128)(2,1)S(1)}, u32[]{:S(2)}, u32[]{:S(2)}) collective-permute-start(bf16[8,64,128]{2,1,0:T(8,128)(2,1)S(1)} %get-tuple-element.26), channel_id=1, source_target_pairs={{0,4},{4,0},{8,12},{12,8},{16,20},{20,16},{24,28},{28,24},{1,5},{5... | collective-permute-start | bytes 393224 | tf_op jit(solution)/shard_map/ppermute | solution.py:28
  47.1 6.8 %collective-permute-start.23 = (bf16[2,4,64,128]{3,2,1,0:T(8,128)(2,1)S(1)}, bf16[2,4,64,128]{3,2,1,0:T(8,128)(2,1)S(1)}, u32[]{:S(2)}, u32[]{:S(2)}) collective-permute-start(bf16[2,4,64,128]{3,2,1,0:T(8,128)(2,1)S(1)} %get-tuple-element.28), channel_id=1, source_target_pairs={{0,24},{4,28},{8,0},{12,4},{16,8},{20,12},{24,16},{28,20},{1,25},{... | collective-permute-start | bytes 393224 | tf_op jit(solution)/shard_map/ppermute | solution.py:23
  49.1 7.1 %collective-permute-start.24 = (bf16[2,4,64,128]{3,2,1,0:T(8,128)(2,1)S(1)}, bf16[2,4,64,128]{3,2,1,0:T(8,128)(2,1)S(1)}, u32[]{:S(2)}, u32[]{:S(2)}) collective-permute-start(bf16[2,4,64,128]{3,2,1,0:T(8,128)(2,1)S(1)} %get-tuple-element.30), channel_id=1, source_target_pairs={{0,24},{4,28},{8,0},{12,4},{16,8},{20,12},{24,16},{28,20},{1,25},{... | collective-permute-start | bytes 393224 | tf_op jit(solution)/shard_map/ppermute | solution.py:23
  51.2 7.9 %collective-permute-start.26 = (bf16[2,4,64,128]{3,2,1,0:T(8,128)(2,1)S(1)}, bf16[2,4,64,128]{3,2,1,0:T(8,128)(2,1)S(1)}, u32[]{:S(2)}, u32[]{:S(2)}) collective-permute-start(bf16[2,4,64,128]{3,2,1,0:T(8,128)(2,1)S(1)} %get-tuple-element.32), channel_id=1, source_target_pairs={{0,24},{4,28},{8,0},{12,4},{16,8},{20,12},{24,16},{28,20},{1,25},{... | collective-permute-start | bytes 393224 | tf_op jit(solution)/shard_map/ppermute | solution.py:23
  51.7 9.3 %collective-permute-start.28 = (bf16[2,4,64,128]{3,2,1,0:T(8,128)(2,1)S(1)}, bf16[2,4,64,128]{3,2,1,0:T(8,128)(2,1)S(1)}, u32[]{:S(2)}, u32[]{:S(2)}) collective-permute-start(bf16[2,4,64,128]{3,2,1,0:T(8,128)(2,1)S(1)} %get-tuple-element.34), channel_id=1, source_target_pairs={{0,24},{4,28},{8,0},{12,4},{16,8},{20,12},{24,16},{28,20},{1,25},{... | collective-permute-start | bytes 393224 | tf_op jit(solution)/shard_map/ppermute | solution.py:23
  52.3 10.3 %collective-permute-start.18 = (bf16[8,64,128]{2,1,0:T(8,128)(2,1)S(1)}, bf16[8,64,128]{2,1,0:T(8,128)(2,1)S(1)}, u32[]{:S(2)}, u32[]{:S(2)}) collective-permute-start(bf16[8,64,128]{2,1,0:T(8,128)(2,1)S(1)} %add_convert_fusion.6), channel_id=1, source_target_pairs={{0,1},{1,0},{2,3},{3,2},{4,5},{5,4},{6,7},{7,6},{8,9},{9,8},{10,11... | collective-permute-start | bytes 393224 | tf_op jit(solution)/shard_map/ppermute | solution.py:18
  53.9 10.2 %collective-permute-start.20 = (bf16[8,64,128]{2,1,0:T(8,128)(2,1)S(1)}, bf16[8,64,128]{2,1,0:T(8,128)(2,1)S(1)}, u32[]{:S(2)}, u32[]{:S(2)}) collective-permute-start(bf16[8,64,128]{2,1,0:T(8,128)(2,1)S(1)} %add_convert_fusion.5), channel_id=1, source_target_pairs={{0,2},{1,3},{2,0},{3,1},{4,6},{5,7},{6,4},{7,5},{8,10},{9,11},{10,... | collective-permute-start | bytes 393224 | tf_op jit(solution)/shard_map/ppermute | solution.py:18
  56.2 7.8 %collective-permute-start.22 = (bf16[8,64,128]{2,1,0:T(8,128)(2,1)S(1)}, bf16[8,64,128]{2,1,0:T(8,128)(2,1)S(1)}, u32[]{:S(2)}, u32[]{:S(2)}) collective-permute-start(bf16[8,64,128]{2,1,0:T(8,128)(2,1)S(1)} %add_convert_fusion.4), channel_id=1, source_target_pairs={{0,3},{1,2},{2,1},{3,0},{4,7},{5,6},{6,5},{7,4},{8,11},{9,10},{10,... | collective-permute-start | bytes 393224 | tf_op jit(solution)/shard_map/ppermute | solution.py:18
  59.0 6.7 %collective-permute-start.25 = (bf16[2,4,64,128]{3,2,1,0:T(8,128)(2,1)S(1)}, bf16[2,4,64,128]{3,2,1,0:T(8,128)(2,1)S(1)}, u32[]{:S(2)}, u32[]{:S(2)}) collective-permute-start(bf16[2,4,64,128]{3,2,1,0:T(8,128)(2,1)S(1)} %add_convert_fusion.2), channel_id=1, source_target_pairs={{0,1},{1,0},{2,3},{3,2},{4,5},{5,4},{6,7},{7,6},{8,9},{9,8},{10,11... | collective-permute-start | bytes 393224 | tf_op jit(solution)/shard_map/ppermute | solution.py:18
  61.0 7.8 %collective-permute-start.27 = (bf16[2,4,64,128]{3,2,1,0:T(8,128)(2,1)S(1)}, bf16[2,4,64,128]{3,2,1,0:T(8,128)(2,1)S(1)}, u32[]{:S(2)}, u32[]{:S(2)}) collective-permute-start(bf16[2,4,64,128]{3,2,1,0:T(8,128)(2,1)S(1)} %add_convert_fusion.1), channel_id=1, source_target_pairs={{0,2},{1,3},{2,0},{3,1},{4,6},{5,7},{6,4},{7,5},{8,10},{9,11},{10,... | collective-permute-start | bytes 393224 | tf_op jit(solution)/shard_map/ppermute | solution.py:18
  62.5 6.2 %collective-permute-start.29 = (bf16[2,4,64,128]{3,2,1,0:T(8,128)(2,1)S(1)}, bf16[2,4,64,128]{3,2,1,0:T(8,128)(2,1)S(1)}, u32[]{:S(2)}, u32[]{:S(2)}) collective-permute-start(bf16[2,4,64,128]{3,2,1,0:T(8,128)(2,1)S(1)} %add_convert_fusion), channel_id=1, source_target_pairs={{0,3},{1,2},{2,1},{3,0},{4,7},{5,6},{6,5},{7,4},{8,11},{9,10},{10,... | collective-permute-start | bytes 393224 | tf_op jit(solution)/shard_map/ppermute | solution.py:18
  (13 other events, 12.4 us)
